TPU v7x, 32 devices: a whole 2x2x4 slice. The times are simulated.
32 devices in a mesh: dp: 8 (over z, y), seq: 4 (over x, core).
Axes of the slice: x: 2, y: 2, z: 4, core: 2. Of those that a mesh axis runs over, the one named last changes fastest.
Arguments:
- tokens: bfloat16 [8, 2048, 768], P('dp', 'seq'), may hold values from -6 to 6
- lengths: int32 [8], P('dp'), may hold values from 512 to 2048, as said below
- qkv_weight: bfloat16 [768, 576], P('dp'), may hold values from -0.4375 to 0.4375
- qv_bias: bfloat16 [1536], P('dp'), may hold values from -0.75 to 0.75
- out_weight: bfloat16 [768, 768], P('dp'), may hold values from -4 to 4
- out_bias: bfloat16 [768], P('dp'), may hold values from -4 to 4
- norm_gain: bfloat16 [768], P('dp'), may hold values from 0.5 to 1.5
- norm_shift: bfloat16 [768], P('dp'), may hold values from -4 to 4
- up_weight: bfloat16 [768, 768], P('dp'), may hold values from -0.4375 to 0.4375
- up_bias: bfloat16 [3072], P('dp'), may hold values from -6 to 6
- down_weight: bfloat16 [3072, 192], P('dp'), may hold values from -0.21875 to 0.21875
- down_bias: bfloat16 [768], P('dp'), may hold values from -4 to 4
- final_gain: bfloat16 [768], P('dp'), may hold values from 0.5 to 1.5
- final_shift: bfloat16 [768], P('dp'), may hold values from -4 to 4
- grad_output: bfloat16 [8, 2048, 768], P('dp', 'seq'), may hold values from -6 to 6
Outputs:
- output: bfloat16 [8, 2048, 768], P('dp', 'seq')
- grad_tokens: bfloat16 [8, 2048, 768], P('dp', 'seq')
- grad_qkv_weight: float32 [768, 576], P('dp')
- grad_qv_bias: float32 [1536], P('dp')
- grad_out_weight: float32 [768, 768], P('dp')
- grad_out_bias: float32 [768], P('dp')
- grad_norm_gain: float32 [768], P('dp')
- grad_norm_shift: float32 [768], P('dp')
- grad_up_weight: float32 [768, 768], P('dp')
- grad_up_bias: float32 [3072], P('dp')
- grad_down_weight: float32 [3072, 192], P('dp')
- grad_down_bias: float32 [768], P('dp')
- grad_final_gain: float32 [768], P('dp')
- grad_final_shift: float32 [768], P('dp')
Inputs may be any that keep to these rules, and one draw needn't show every extreme that they name: `lengths`: tokens at positions below the length are valid, the rest of the 2048 slots are padding; some sequence is full and some has 512.
All inputs are finite; a program needn't handle non-finite values.
Results may differ from a plain program's by a relative error of at most 0.015.
Values may be sent and summed in bfloat16 or wider, within the bound.
A program may use at most 128 MiB of HBM per device.

v0:
```python
import jax
import jax.numpy as jnp
from jax import lax
from jax.sharding import PartitionSpec as P

H = 12
GROUPS = 4
HD = 64
QB = 512


epsilon = 1e-05
masked_score = -1000000000.0


def norm_rows(values, scales, shifts):
    row_mean = jnp.mean(values, axis=-1, keepdims=True)
    centred = values - row_mean
    row_var = jnp.mean(centred * centred, axis=-1, keepdims=True)
    return centred * lax.rsqrt(row_var + epsilon) * scales + shifts


def exact_gelu(values):
    return jax.nn.gelu(values, approximate=False)


def group_mult(values, matrix):
    return jnp.einsum("ngi,gio->ngo", values, matrix, preferred_element_type=jnp.float32)


def group_back(grads, matrix):
    return jnp.einsum("ngo,gio->ngi", grads, matrix, preferred_element_type=jnp.float32)


def group_outer(values, grads):
    return jnp.einsum("ngi,ngo->gio", values, grads, preferred_element_type=jnp.float32)


def on_device(
    tokens,
    lengths,
    qkv_weight,
    qv_bias,
    out_weight,
    out_bias,
    norm_gain,
    norm_shift,
    up_weight,
    up_bias,
    down_weight,
    down_bias,
    final_gain,
    final_shift,
    grad_output,
):
    seq_count, piece_rows, model_width = tokens.shape
    tok_rows = seq_count * piece_rows
    group_width = model_width // GROUPS
    hidden_group = up_weight.shape[1]
    heads_here = H // lax.axis_size("seq")
    score_scale = HD ** (-0.5)
    attention_full = (
        lax.all_gather(qkv_weight, "dp", axis=0, tiled=True),
        lax.all_gather(qv_bias, "dp", axis=0, tiled=True),
        lax.all_gather(out_weight, "dp", axis=0, tiled=True),
        lax.all_gather(out_bias, "dp", axis=0, tiled=True),
        lax.all_gather(norm_gain, "dp", axis=0, tiled=True),
        lax.all_gather(norm_shift, "dp", axis=0, tiled=True),
    )
    feed_full = (
        lax.all_gather(up_weight, "dp", axis=0, tiled=True),
        lax.all_gather(up_bias, "dp", axis=0, tiled=True),
        lax.all_gather(down_weight, "dp", axis=0, tiled=True),
        lax.all_gather(down_bias, "dp", axis=0, tiled=True),
        lax.all_gather(final_gain, "dp", axis=0, tiled=True),
        lax.all_gather(final_shift, "dp", axis=0, tiled=True),
    )
    qkv_full, qv_full, out_full, obias_full, gain_one, shift_one = attention_full
    up_full, upb_full, down_full, downb_full, gain_two, shift_two = feed_full
    token_groups = tokens.reshape(tok_rows, GROUPS, group_width)
    mixed_qkv = group_mult(token_groups, qkv_full.reshape(GROUPS, group_width, 3 * group_width))
    mixed_qkv = mixed_qkv.reshape(tok_rows, GROUPS, 3, group_width)
    bias_float = qv_full.astype(jnp.float32)
    bias_block = jnp.stack(
        [
            bias_float[:model_width].reshape(GROUPS, group_width),
            jnp.zeros((GROUPS, group_width), jnp.float32),
            bias_float[model_width:].reshape(GROUPS, group_width),
        ],
        axis=1,
    )
    projected = (mixed_qkv + bias_block).astype(jnp.bfloat16)
    by_heads = lax.all_to_all(
        projected.reshape(seq_count, piece_rows, GROUPS, 3, group_width),
        "seq",
        split_axis=2,
        concat_axis=1,
        tiled=True,
    )
    slot_len = by_heads.shape[1]
    block_count = slot_len // QB
    query_heads = by_heads[:, :, 0, 0].reshape(seq_count, slot_len, heads_here, HD)
    key_heads = by_heads[:, :, 0, 1].reshape(seq_count, slot_len, heads_here, HD)
    value_heads = by_heads[:, :, 0, 2].reshape(seq_count, slot_len, heads_here, HD)
    positions = jnp.arange(slot_len, dtype=jnp.int32)
    block_index = jnp.arange(block_count, dtype=jnp.int32)

    def block_scores(block_query, key_rows, valid_keys):
        scores = (
            jnp.einsum("qhd,khd->hqk", block_query, key_rows, preferred_element_type=jnp.float32)
            * score_scale
        )
        return jnp.where(valid_keys[None, None, :], scores, masked_score)

    def attend_sequence(sequence):
        query_rows, key_rows, value_rows, seq_length = sequence
        valid_keys = positions < seq_length

        def attend_block(index_now):
            block_query = lax.dynamic_slice_in_dim(query_rows, index_now * QB, QB, 0)
            scores = block_scores(block_query, key_rows, valid_keys)
            row_max = jnp.max(scores, axis=-1, keepdims=True)
            exponent = jnp.exp(scores - row_max)
            row_total = jnp.sum(exponent, axis=-1, keepdims=True)
            weights = (exponent / row_total).astype(jnp.bfloat16)
            context = jnp.einsum(
                "hqk,khd->qhd", weights, value_rows, preferred_element_type=jnp.float32
            )
            return (context.astype(jnp.bfloat16), (row_max + jnp.log(row_total))[:, :, 0])

        context, log_totals = lax.map(attend_block, block_index)
        return (context.reshape(slot_len, heads_here * HD), log_totals)

    context_heads, log_totals = lax.map(
        attend_sequence, (query_heads, key_heads, value_heads, lengths)
    )
    context_back = lax.all_to_all(
        context_heads.reshape(seq_count, slot_len, 1, group_width),
        "seq",
        split_axis=1,
        concat_axis=2,
        tiled=True,
    )
    context_tok = context_back.reshape(tok_rows, model_width)
    attended = jnp.dot(
        context_tok, out_full, preferred_element_type=jnp.float32
    ) + obias_full.astype(jnp.float32)
    resid_one = tokens.reshape(tok_rows, model_width).astype(jnp.float32) + attended
    mixed, pull_one = jax.vjp(
        norm_rows, resid_one, gain_one.astype(jnp.float32), shift_one.astype(jnp.float32)
    )
    mixed_low = mixed.astype(jnp.bfloat16)
    upper = group_mult(
        mixed_low.reshape(tok_rows, GROUPS, group_width),
        up_full.reshape(GROUPS, group_width, hidden_group),
    ).reshape(tok_rows, -1)
    upper = upper + upb_full.astype(jnp.float32)
    active_full, pull_gelu = jax.vjp(exact_gelu, upper)
    active = active_full.astype(jnp.bfloat16)
    lowered = group_mult(
        active.reshape(tok_rows, GROUPS, hidden_group),
        down_full.reshape(GROUPS, hidden_group, group_width),
    ).reshape(tok_rows, model_width)
    lowered = lowered + downb_full.astype(jnp.float32)
    normed, pull_two = jax.vjp(
        norm_rows, mixed + lowered, gain_two.astype(jnp.float32), shift_two.astype(jnp.float32)
    )
    token_pos = lax.axis_index("seq") * piece_rows + jnp.arange(piece_rows, dtype=jnp.int32)
    token_mask = (token_pos[None, :] < lengths[:, None]).reshape(tok_rows, 1).astype(jnp.float32)
    output = (normed * token_mask).astype(jnp.bfloat16).reshape(seq_count, piece_rows, model_width)
    feed_full = (
        lax.all_gather(up_weight, "dp", axis=0, tiled=True),
        lax.all_gather(up_bias, "dp", axis=0, tiled=True),
        lax.all_gather(down_weight, "dp", axis=0, tiled=True),
        lax.all_gather(down_bias, "dp", axis=0, tiled=True),
        lax.all_gather(final_gain, "dp", axis=0, tiled=True),
        lax.all_gather(final_shift, "dp", axis=0, tiled=True),
    )
    up_full, upb_full, down_full, downb_full, gain_two, shift_two = feed_full
    grad_normed = grad_output.reshape(tok_rows, model_width).astype(jnp.float32) * token_mask
    grad_resid_two, grad_final_gain, grad_final_shift = pull_two(grad_normed)
    grad_down_bias = jnp.sum(grad_resid_two, axis=0)
    grad_lowered = grad_resid_two.astype(jnp.bfloat16).reshape(tok_rows, GROUPS, group_width)
    grad_down_weight = group_outer(active.reshape(tok_rows, GROUPS, hidden_group), grad_lowered)
    grad_down_weight = grad_down_weight.reshape(-1, group_width)
    grad_active = group_back(grad_lowered, down_full.reshape(GROUPS, hidden_group, group_width))
    (grad_upper,) = pull_gelu(grad_active.reshape(tok_rows, -1))
    grad_up_bias = jnp.sum(grad_upper, axis=0)
    grad_up_low = grad_upper.astype(jnp.bfloat16).reshape(tok_rows, GROUPS, hidden_group)
    grad_up_weight = group_outer(mixed_low.reshape(tok_rows, GROUPS, group_width), grad_up_low)
    grad_up_weight = grad_up_weight.reshape(-1, hidden_group)
    grad_mixed = group_back(grad_up_low, up_full.reshape(GROUPS, group_width, hidden_group))
    grad_mixed = grad_mixed.reshape(tok_rows, model_width) + grad_resid_two
    grad_resid_one, grad_norm_gain, grad_norm_shift = pull_one(grad_mixed)
    feed_grads = (
        lax.psum_scatter(grad_up_weight, "dp", scatter_dimension=0, tiled=True),
        lax.psum_scatter(grad_up_bias, "dp", scatter_dimension=0, tiled=True),
        lax.psum_scatter(grad_down_weight, "dp", scatter_dimension=0, tiled=True),
        lax.psum_scatter(grad_down_bias, "dp", scatter_dimension=0, tiled=True),
        lax.psum_scatter(grad_final_gain, "dp", scatter_dimension=0, tiled=True),
        lax.psum_scatter(grad_final_shift, "dp", scatter_dimension=0, tiled=True),
    )
    attention_full = (
        lax.all_gather(qkv_weight, "dp", axis=0, tiled=True),
        lax.all_gather(qv_bias, "dp", axis=0, tiled=True),
        lax.all_gather(out_weight, "dp", axis=0, tiled=True),
        lax.all_gather(out_bias, "dp", axis=0, tiled=True),
        lax.all_gather(norm_gain, "dp", axis=0, tiled=True),
        lax.all_gather(norm_shift, "dp", axis=0, tiled=True),
    )
    qkv_full, qv_full, out_full, obias_full, gain_one, shift_one = attention_full
    grad_out_bias = jnp.sum(grad_resid_one, axis=0)
    grad_attended = grad_resid_one.astype(jnp.bfloat16)
    grad_out_weight = jnp.einsum(
        "nc,nd->cd", context_tok, grad_attended, preferred_element_type=jnp.float32
    )
    grad_context = jnp.einsum(
        "nd,cd->nc", grad_attended, out_full, preferred_element_type=jnp.float32
    ).astype(jnp.bfloat16)
    grad_context_heads = lax.all_to_all(
        grad_context.reshape(seq_count, piece_rows, GROUPS, group_width),
        "seq",
        split_axis=2,
        concat_axis=1,
        tiled=True,
    )
    grad_context_heads = grad_context_heads.reshape(seq_count, slot_len, heads_here, HD)

    def revisit_sequence(sequence):
        query_rows, key_rows, value_rows, grad_rows, lse_rows, seq_length = sequence
        valid_keys = positions < seq_length

        def revisit_block(carried, index_now):
            key_sum, value_sum = carried
            block_query = lax.dynamic_slice_in_dim(query_rows, index_now * QB, QB, 0)
            block_grad = lax.dynamic_slice_in_dim(grad_rows, index_now * QB, QB, 0)
            block_lse = lax.dynamic_index_in_dim(lse_rows, index_now, 0, keepdims=False)
            scores = block_scores(block_query, key_rows, valid_keys)
            probs = jnp.exp(scores - block_lse[:, :, None])
            weights = probs.astype(jnp.bfloat16)
            value_sum = value_sum + jnp.einsum(
                "hqk,qhd->khd", weights, block_grad, preferred_element_type=jnp.float32
            )
            grad_probs = jnp.einsum(
                "qhd,khd->hqk", block_grad, value_rows, preferred_element_type=jnp.float32
            )
            inner_sum = jnp.sum(probs * grad_probs, axis=-1, keepdims=True)
            grad_scores = (probs * (grad_probs - inner_sum)).astype(jnp.bfloat16)
            grad_query = (
                jnp.einsum(
                    "hqk,khd->qhd", grad_scores, key_rows, preferred_element_type=jnp.float32
                )
                * score_scale
            )
            key_sum = (
                key_sum
                + jnp.einsum(
                    "hqk,qhd->khd", grad_scores, block_query, preferred_element_type=jnp.float32
                )
                * score_scale
            )
            return ((key_sum, value_sum), grad_query.astype(jnp.bfloat16))

        zero_rows = jnp.zeros((slot_len, heads_here, HD), jnp.float32)
        (key_sum, value_sum), grad_queries = lax.scan(
            revisit_block, (zero_rows, zero_rows), block_index
        )
        return jnp.stack(
            [
                grad_queries.reshape(slot_len, -1),
                key_sum.reshape(slot_len, -1).astype(jnp.bfloat16),
                value_sum.reshape(slot_len, -1).astype(jnp.bfloat16),
            ],
            axis=1,
        )

    grad_heads = lax.map(
        revisit_sequence,
        (query_heads, key_heads, value_heads, grad_context_heads, log_totals, lengths),
    )
    grad_proj = lax.all_to_all(
        grad_heads.reshape(seq_count, slot_len, 1, 3, group_width),
        "seq",
        split_axis=1,
        concat_axis=2,
        tiled=True,
    )
    grad_proj = grad_proj.reshape(tok_rows, GROUPS, 3 * group_width)
    grad_qkv_weight = group_outer(token_groups, grad_proj).reshape(-1, 3 * group_width)
    bias_sums = jnp.sum(grad_proj, axis=0, dtype=jnp.float32).reshape(GROUPS, 3, group_width)
    grad_qv_bias = jnp.concatenate([bias_sums[:, 0].reshape(-1), bias_sums[:, 2].reshape(-1)])
    grad_inputs = group_back(grad_proj, qkv_full.reshape(GROUPS, group_width, 3 * group_width))
    grad_tokens = (grad_inputs.reshape(tok_rows, model_width) + grad_resid_one).astype(jnp.bfloat16)
    grad_tokens = grad_tokens.reshape(seq_count, piece_rows, model_width)
    attention_grads = (
        lax.psum_scatter(grad_qkv_weight, "dp", scatter_dimension=0, tiled=True),
        lax.psum_scatter(grad_qv_bias, "dp", scatter_dimension=0, tiled=True),
        lax.psum_scatter(grad_out_weight, "dp", scatter_dimension=0, tiled=True),
        lax.psum_scatter(grad_out_bias, "dp", scatter_dimension=0, tiled=True),
        lax.psum_scatter(grad_norm_gain, "dp", scatter_dimension=0, tiled=True),
        lax.psum_scatter(grad_norm_shift, "dp", scatter_dimension=0, tiled=True),
    )
    summed = (
        lax.psum(attention_grads[0].astype(jnp.bfloat16), "seq").astype(jnp.float32),
        lax.psum(attention_grads[1].astype(jnp.bfloat16), "seq").astype(jnp.float32),
        lax.psum(attention_grads[2].astype(jnp.bfloat16), "seq").astype(jnp.float32),
        lax.psum(attention_grads[3].astype(jnp.bfloat16), "seq").astype(jnp.float32),
        lax.psum(attention_grads[4].astype(jnp.bfloat16), "seq").astype(jnp.float32),
        lax.psum(attention_grads[5].astype(jnp.bfloat16), "seq").astype(jnp.float32),
        lax.psum(feed_grads[0].astype(jnp.bfloat16), "seq").astype(jnp.float32),
        lax.psum(feed_grads[1].astype(jnp.bfloat16), "seq").astype(jnp.float32),
        lax.psum(feed_grads[2].astype(jnp.bfloat16), "seq").astype(jnp.float32),
        lax.psum(feed_grads[3].astype(jnp.bfloat16), "seq").astype(jnp.float32),
        lax.psum(feed_grads[4].astype(jnp.bfloat16), "seq").astype(jnp.float32),
        lax.psum(feed_grads[5].astype(jnp.bfloat16), "seq").astype(jnp.float32),
    )
    return (
        output,
        grad_tokens,
        summed[0],
        summed[1],
        summed[2],
        summed[3],
        summed[4],
        summed[5],
        summed[6],
        summed[7],
        summed[8],
        summed[9],
        summed[10],
        summed[11],
    )


def solution(mesh):
    in_specs = (
        P("dp", "seq", None),
        P("dp"),
        P("dp", None),
        P("dp"),
        P("dp", None),
        P("dp"),
        P("dp"),
        P("dp"),
        P("dp", None),
        P("dp"),
        P("dp", None),
        P("dp"),
        P("dp"),
        P("dp"),
        P("dp", "seq", None),
    )
    out_specs = (
        P("dp", "seq", None),
        P("dp", "seq", None),
        P("dp", None),
        P("dp"),
        P("dp", None),
        P("dp"),
        P("dp"),
        P("dp"),
        P("dp", None),
        P("dp"),
        P("dp", None),
        P("dp"),
        P("dp"),
        P("dp"),
    )
    return jax.shard_map(
        on_device, mesh=mesh, in_specs=in_specs, out_specs=out_specs, check_vma=False
    )
```

profile of v0, /device:TPU:0, one launch (start us, length us, event | category | flops | bytes accessed | tf_op | source)
XLA Modules:
  0.0 654.5 jit_solution(4067557235894084284)
XLA Ops:
  16.4 39.3 %all-reduce.16 = (bf16[1536]{0:T(1024)(128)(2,1)S(1)}, bf16[768]{0:T(1024)(128)(2,1)S(1)}, bf16[768]{0:T(1024)(128)(2,1)S(1)}, bf16[768]{0:T(1024)(128)(2,1)S(1)...) all-reduce(bf16[1536]{0:T(1024)(128)(2,1)S(1)} %dynamic-update-slic, ...), channel_id=1, replica_groups=mesh['dp'=8,'seq'=4] {'dp'}, use_global_device_ids=true, to_apply=%add | all-reduce | flops 6144 | bytes 24576
  57.5 32.3 %all_gather.40 = bf16[768,576]{1,0:T(8,128)(2,1)S(1)} all-gather(bf16[96,576]{1,0:T(8,128)(2,1)} %param.21), channel_id=1, replica_groups=mesh['dp'=8,'seq'=4] {'dp'}, dimensions={0}, use_global_device_ids=true | all-gather | bytes 995328 | tf_op jit(solution)/shard_map/all_gather | solution.py:63
  92.6 3.6 all-to-all-start
  97.0 27.7 %all-to-all-done = bf16[1,512,4,3,192]{1,4,3,0,2:T(8,128)(2,1)S(1)} async-done(((bf16[1,512,4,3,192]{1,4,3,0,2:T(8,128)(2,1)}), bf16[1,512,4,3,192]{1,4,3,0,2:T(8,128)(2,1)S(1)}, u32[]{:S(2)}, u32[]{:S(2)}) %all-to-all-start) | async-done | bytes 2359328 | tf_op jit(solution)/shard_map/all_to_all | solution.py:93
  125.3 41.8 %while.46 = (s32[]{:T(128)}, bf16[4,512,3,64]{1,3,2,0:T(8,128)(2,1)S(1)}, f32[4,3,512]{2,1,0:T(4,128)S(1)}, s32[4]{0:T(128)S(1)}, bf16[2048,3,64]{0,2,1:T(8,128)...) while((s32[]{:T(128)}, ...), condition=%wide.region_3.4_spmd.clone, body=%wide.region_0.3_spmd.clone.sunk | while | flops 843153920 | bytes 39782596 | solution.py:131
  132.0 3.7 fusion.148
  142.4 3.7 fusion.148
  152.9 3.7 fusion.148
  163.3 3.7 fusion.148
  170.6 3.8 copy.99
  174.9 13.7 %reduce.4 = bf16[2048,192]{1,0:T(8,128)(2,1)} reduce(bf16[2048,1,1,192]{3,2,1,0:T(2,128)(2,1)} %bitcast.269, bf16[]{:T(256)} %broadcast.359), dimensions={1,2}, to_apply=%bitcast.191.reduce_sub_computation | reduce | bytes 1572866
  188.6 3.9 reshape.381
  192.5 3.5 all-to-all-start.1
  197.5 26.6 %all-gather = bf16[8,1,384]{2,1,0:T(2,128)(2,1)S(1)} all-gather(bf16[1,1,384]{2,1,0:T(2,128)(2,1)S(1)} %reshape.353), channel_id=1, replica_groups=mesh['dp'=8,'seq'=4] {'dp'}, dimensions={0}, use_global_device_ids=true | all-gather | bytes 6912 | tf_op jit(solution)/shard_map/all_gather | solution.py:72
  226.8 4.5 copy.100
  239.5 18.0 %fusion.50 = (bf16[512,4,768]{2,0,1:T(8,128)(2,1)}, f32[512,4,768]{2,0,1:T(8,128)}, f32[4,512,768]{2,1,0:T(8,128)}) fusion(f32[4,768]{1,0:T(4,128)S(1)} %reshape.330, bf16[512,4,192]{0,2,1:T(8,128)(2,1)} %bitcast.277, bf16[4,192,768]{2,1,0:T(8,128)(2,1)} %bitcast.286), kind=kOutput, calls=%fused_computation.63 | convolution fusion | flops 707788800 | bytes 17707008 | tf_op jit(solution)/shard_map/ngi,gio->ngo/dot_general | solution.py:28
  257.5 4.5 fusion.76
  262.0 3.1 copy.104
  280.6 9.4 %fusion.95 = (f32[4,768]{1,0:T(4,128)}, bf16[512,4,768]{2,0,1:T(8,128)(2,1)S(1)}) fusion(f32[512,4,768]{2,0,1:T(8,128)} %get-tuple-element.315, bf16[512,4,192]{0,2,1:T(8,128)(2,1)} %bitcast.280, bf16[24,4,8,768]{3,2,1,0:T(8,128)(2,1)} %bitcast.289, f32[4,512,768]{2,1,0:T(8,128)} %get-tuple-element.336, f32[4,768]{1,0:T(4,128)S(1)} %reshape.330), kind=kOutput, calls=%fused_computation.150 | convolution fusion | flops 629142528 | bytes 17719296 | tf_op jit(solution)/shard_map/ngo,gio->ngi/dot_general | solution.py:32
  293.9 4.6 fusion.72
  298.5 3.1 copy.107
  301.5 3.3 multiply_reduce_fusion.1
  308.7 4.2 all-to-all-start.2
  313.0 3.9 fusion.85
  317.0 7.6 %all-to-all-done.2 = bf16[1,512,4,192]{1,3,0,2:T(8,128)(2,1)} async-done(((bf16[1,512,4,192]{1,3,0,2:T(8,128)(2,1)}), bf16[1,512,4,192]{1,3,0,2:T(8,128)(2,1)}, u32[]{:S(2)}, u32[]{:S(2)}) %all-to-all-start.2) | async-done | bytes 786464 | tf_op jit(solution)/shard_map/all_to_all | solution.py:220
  331.2 119.7 %while.47 = (s32[]{:T(128)}, f32[2048,3,64]{0,2,1:T(8,128)S(1)}, f32[2048,3,64]{0,2,1:T(8,128)}, bf16[4,512,3,64]{1,3,2,0:T(8,128)(2,1)}, s32[4]{0:T(128)S(1)}, ...) while((s32[]{:T(128)}, f32[2048,3,64]{0,2,1:T(8,128)S(1)}, ...), condition=%wide.region_14.15_spmd.clone, body=%wide.region_12.14_spmd.clone.sunk | while | flops 2062615040 | bytes 129222968 | solution.py:265
  337.8 4.9 fusion.160
  342.7 4.8 multiply_reduce_fusion.6
  347.6 5.0 multiply_convert_fusion.3
  352.6 5.6 fusion.161
  367.2 5.5 fusion.160
  372.8 4.8 multiply_reduce_fusion.6
  377.6 5.0 multiply_convert_fusion.3
  382.6 5.7 fusion.161
  397.3 5.5 fusion.160
  402.9 4.8 multiply_reduce_fusion.6
  407.7 5.0 multiply_convert_fusion.3
  412.7 5.7 fusion.161
  427.4 5.5 fusion.160
  432.9 4.8 multiply_reduce_fusion.6
  437.8 5.0 multiply_convert_fusion.3
  442.7 5.8 fusion.161
  455.2 5.0 copy.112
  460.2 53.8 %all_to_all.63 = bf16[1,2048,1,3,192]{4,3,2,0,1:T(4,128)(2,1)} all-to-all(bf16[1,2048,1,3,192]{4,3,2,0,1:T(4,128)(2,1)} %copy.112), channel_id=1, replica_groups=mesh['dp'=8,'seq'=4] {'seq'}, dimensions={1} | all-to-all | bytes 4718592 | tf_op jit(solution)/shard_map/all_to_all | solution.py:281
  514.0 7.4 %copy.119 = bf16[1,4,512,1,3,192]{2,1,5,4,3,0:T(4,128)(2,1)} copy(bf16[1,4,512,1,3,192]{5,4,2,1,3,0:T(4,128)(2,1)} %bitcast.262) | data formatting | bytes 4718592 | tf_op jit(solution)/shard_map/all_to_all | solution.py:281
  538.3 52.0 %reduce-scatter.5.cloned.1.call-done = f32[96,576]{1,0:T(8,128)} async-done(((f32[768,576]{1,0:T(8,128)}), f32[96,576]{1,0:T(8,128)}) %reduce-scatter.5.cloned.1.call-update) | async-done | bytes 221200 | tf_op jit(solution)/shard_map/reduce_scatter | solution.py:296
  595.1 35.2 %all-reduce.15 = (bf16[1536]{0:T(1024)(128)(2,1)S(1)}, bf16[768]{0:T(1024)(128)(2,1)S(1)}, bf16[768]{0:T(1024)(128)(2,1)S(1)}, bf16[768]{0:T(1024)(128)(2,1)S(1)...) all-reduce(f32[1536]{0:T(1024)S(1)} %pad_maximum_fusion.1, ...), channel_id=3, replica_groups=mesh['dp'=8,'seq'=4] {'dp'}, use_global_device_ids=true, to_apply=%region_18.19.clone | all-reduce | flops 9216 | bytes 55296
  630.9 5.7 all-reduce.17
  (231 shorter events, 144.0 us)
Async XLA Ops:
  7.2 225.8 %all-gather.5.cloned.1.call-start = ((), (), s32[]{:S(2)}) async-start(), calls=%async_computation.8 | async-start | bytes 1327104 | tf_op jit(solution)/shard_map/all_gather | solution.py:65
  57.5 33.1 %copy-start.8 = (bf16[1,512,768]{1,2,0:T(8,128)(2,1)}, bf16[1,512,768]{1,2,0:T(8,128)(2,1)S(1)}, u32[]{:S(2)}) copy-start(bf16[1,512,768]{1,2,0:T(8,128)(2,1)S(1)} %copy.94) | copy-start | bytes 2359300
  89.8 1.0 copy-start.6
  92.6 32.1 %all-to-all-start = ((bf16[1,512,4,3,192]{1,4,3,0,2:T(8,128)(2,1)}), bf16[1,512,4,3,192]{1,4,3,0,2:T(8,128)(2,1)S(1)}, u32[]{:S(2)}, u32[]{:S(2)}) async-start(bf16[1,512,4,3,192]{1,4,3,0,2:T(8,128)(2,1)} %add_convert_fusion), calls=%async_computation | async-start | bytes 4718592 | tf_op jit(solution)/shard_map/all_to_all | solution.py:93
  96.2 143.3 %all-gather.7.cloned.1.call-start = ((), (), s32[]{:S(2)}) async-start(), calls=%async_computation.9 | async-start | bytes 1327104 | tf_op jit(solution)/shard_map/all_gather | solution.py:71
  167.0 21.5 %copy-start.2 = (bf16[2048,3,64]{0,2,1:T(8,128)(2,1)}, bf16[2048,3,64]{0,2,1:T(8,128)(2,1)S(1)}, u32[]{:S(2)}) copy-start(bf16[2048,3,64]{0,2,1:T(8,128)(2,1)S(1)} %get-tuple-element.566) | copy-start | bytes 2359300
  174.9 22.5 %copy-start.20 = (bf16[384]{0:T(512)(128)(2,1)S(1)}, bf16[384]{0:T(512)(128)(2,1)}, u32[]{:S(2)}) copy-start(bf16[384]{0:T(512)(128)(2,1)} %param.28) | copy-start | bytes 2308
  192.5 31.7 %all-to-all-start.1 = ((bf16[4,2,49152]{2,1,0:T(2,128)(2,1)}), bf16[4,2,49152]{2,1,0:T(2,128)(2,1)S(1)}, u32[]{:S(2)}, u32[]{:S(2)}) async-start(bf16[4,2,49152]{2,1,0:T(2,128)(2,1)} %reshape.381), calls=%async_computation.1 | async-start | bytes 1572864 | tf_op jit(solution)/shard_map/all_to_all | solution.py:137
  196.0 61.5 %all-gather.9.cloned.1.call-start = ((), (), s32[]{:S(2)}) async-start(), calls=%async_computation.10 | async-start | bytes 1327104 | tf_op jit(solution)/shard_map/all_gather | solution.py:73
  196.7 336.5 %reduce-scatter.11.cloned.1.call-start = ((), (), s32[]{:S(2)}) async-start(), calls=%async_computation.14 | async-start | bytes 2654208 | tf_op jit(solution)/shard_map/reduce_scatter | solution.py:198
  265.1 2.4 copy-start.11
  270.5 1.1 copy-start.5
  280.3 254.7 %reduce-scatter.9.cloned.1.call-start = ((), (), s32[]{:S(2)}) async-start(), calls=%async_computation.13 | async-start | bytes 2654208 | tf_op jit(solution)/shard_map/reduce_scatter | solution.py:196
  280.6 11.1 %copy-start.10 = (bf16[512,768]{0,1:T(8,128)(2,1)S(1)}, bf16[512,768]{0,1:T(8,128)(2,1)}, u32[]{:S(2)}) copy-start(bf16[512,768]{0,1:T(8,128)(2,1)} %copy.102) | copy-start | bytes 2359300
  289.9 1.7 copy-start.1
  304.8 1.8 copy-start.21
  305.5 1.2 copy-start.3
  305.5 7.5 %copy-start.12 = (f32[512]{0:T(512)}, f32[512]{0:T(512)S(1)}, u32[]{:S(2)}) copy-start(f32[512]{0:T(512)S(1)} %negate_multiply_fusion.1) | copy-start | bytes 6148
  308.7 15.9 %all-to-all-start.2 = ((bf16[1,512,4,192]{1,3,0,2:T(8,128)(2,1)}), bf16[1,512,4,192]{1,3,0,2:T(8,128)(2,1)}, u32[]{:S(2)}, u32[]{:S(2)}) async-start(bf16[1,512,4,192]{1,3,0,2:T(8,128)(2,1)} %bitcast.29), calls=%async_computation.2 | async-start | bytes 1572864 | tf_op jit(solution)/shard_map/all_to_all | solution.py:220
  312.9 223.8 %reduce-scatter.7.cloned.1.call-start = ((), (), s32[]{:S(2)}) async-start(), calls=%async_computation.12 | async-start | bytes 2654208 | tf_op jit(solution)/shard_map/reduce_scatter | solution.py:298
  317.0 273.4 %reduce-scatter.5.cloned.1.call-start = ((), (), s32[]{:S(2)}) async-start(), calls=%async_computation.11 | async-start | bytes 2211840 | tf_op jit(solution)/shard_map/reduce_scatter | solution.py:296
  352.6 5.6 copy-start
  382.6 5.8 copy-start
  412.7 5.7 copy-start
  442.7 5.8 copy-start
  521.4 2.2 copy-start.9
  523.7 4.4 copy-start.19
  526.0 5.3 copy-start.7
  526.0 114.8 %all-reduce.21.cloned.1.call-start = ((), (), s32[]{:S(2)}) async-start(), calls=%async_computation.15 | async-start | bytes 1130496 | tf_op jit(solution)/shard_map/psum | solution.py:304
  533.3 60.6 %copy-start.4 = (f32[512,768]{1,0:T(8,128)S(1)}, f32[512,768]{1,0:T(8,128)}, u32[]{:S(2)}) copy-start(f32[512,768]{1,0:T(8,128)} %copy-done.3) | copy-start | bytes 4718596
  533.3 60.6 %copy-start.13 = (f32[512]{0:T(512)S(1)}, f32[512]{0:T(512)}, u32[]{:S(2)}) copy-start(f32[512]{0:T(512)} %copy-done.12) | copy-start | bytes 6148
  592.0 3.1 copy-start.14
  592.0 3.1 copy-start.15
  592.0 3.1 copy-start.16
  592.0 3.1 copy-start.17
  592.0 3.1 copy-start.18
Sparse Core Ops, SparseCore 0:
  10.2 43.7 all-gather.4
  99.2 38.8 all-gather.6
  198.9 38.1 all-gather.8
  280.5 67.2 reduce-scatter.10
  351.1 69.0 reduce-scatter.8
  423.5 68.9 reduce-scatter.6
  526.1 64.1 reduce-scatter.4
  594.0 32.7 all-reduce.20
where the time goes:
time: 660 us; the launch traced here: 655 us
  blocking collectives  193 us (29%)
  matrix products  161 us (24%)
  waiting for transfers between devices  89.1 us (14%)
  other arithmetic  87.8 us (13%)
  local copies, waits for them, and re-layouts  79 us (12%)
  between operations  18.9 us (3%)
  loops' own time  13.4 us (2%)
  starting transfers between devices  12.1 us (2%)
    unnamed x2, blocking collectives  74.6 us
    all_to_all x1, blocking collectives, on_device(): lax.all_to_all(grad_heads.reshape(seq_count, slot_len, 1, 3, group_width)...  53.8 us
    reduce_scatter x1, waiting for transfers between devices, on_device(): lax.psum_scatter(grad_qkv_weight, 'dp', scatter_dimension=0, tiled=True)  52 us
    all_gather x1, blocking collectives, on_device(): lax.all_gather(qkv_weight, 'dp', axis=0, tiled=True)  32.3 us
    all_to_all x1, waiting for transfers between devices, on_device(): lax.all_to_all(projected.reshape(seq_count, piece_rows, GROUPS, 3, group_...  27.7 us
    all_gather x1, blocking collectives, on_device(): lax.all_gather(up_bias, 'dp', axis=0, tiled=True)  26.6 us
    dot_general x3, matrix products, group_mult(): jnp.einsum('ngi,gio->ngo', values, matrix, preferred_element_type=jnp.flo...  23.4 us
    dot_general x4, matrix products, revisit_block(): jnp.einsum('hqk,khd->qhd', grad_scores, key_rows, preferred_element_type=...  22.9 us
  transfers between devices with their start and end apart: 11, of which 3 were waited for; matrix products, arithmetic and copies ran while one was open for 45% of the time, Pallas kernels for 0%

commit v1 on v0

v1 whole, which is shorter than its diff:
```python
import functools

import jax
import jax.numpy as jnp
from jax import lax
from jax.experimental import pallas as pl
from jax.experimental.pallas import tpu as pltpu
from jax.sharding import PartitionSpec as P

H = 12
GROUPS = 4
HD = 64
epsilon = 1e-05
LOG2E = 1.4426950408889634
MASKED = -1e30
F32 = jnp.float32
BF16 = jnp.bfloat16


def mm(a, b):
    return jnp.dot(a, b, preferred_element_type=F32)


def mm_nt(a, b):
    return lax.dot_general(a, b, (((1,), (1,)), ((), ())), preferred_element_type=F32)


def mm_tn(a, b):
    return lax.dot_general(a, b, (((0,), (0,)), ((), ())), preferred_element_type=F32)


def pad_rows(w, half):
    zeros = jnp.zeros((64, w.shape[1]), w.dtype)
    return jnp.concatenate([w, zeros] if half == 0 else [zeros, w], axis=0)


def pad_lanes(w, half):
    zeros = jnp.zeros((w.shape[0], 64), w.dtype)
    return jnp.concatenate([w, zeros] if half == 0 else [zeros, w], axis=1)


def window(half):
    return slice(half * 128, half * 128 + 256)


def attend_kernel(len_ref, x_ref, w_ref, b_ref, ctx_ref, linv_ref, e_ref, k_out, qT_out, vT_out, qe, ke, ve):
    heads = qe.shape[0]
    sources, rows, _ = x_ref.shape
    gw = heads * HD
    slot = sources * 2 * rows

    @pl.when(pl.program_id(0) == 0)
    def _():
        scale = HD ** (-0.5) * LOG2E
        lane = lax.broadcasted_iota(jnp.int32, (slot, 128), 1)
        ones_lane = jnp.where(lane == 0, 1.0, 0.0).astype(BF16)
        key_pos = lax.broadcasted_iota(jnp.int32, (128, slot), 1)
        key_row = lax.broadcasted_iota(jnp.int32, (128, slot), 0)
        bias = jnp.where((key_row == 0) & (key_pos >= len_ref[0]), MASKED, 0.0).astype(BF16)
        for h in range(heads):
            qe[h, :, 128:256] = ones_lane
            ke[h, 128:256, :] = bias
        for s in range(sources):
            for half in range(2):
                at = (s * 2 + half) * rows
                w = pad_rows(w_ref[...], half)
                qkv = (mm(x_ref[s, :, window(half)], w) + b_ref[...]).astype(BF16)
                q = qkv[:, :gw]
                k = qkv[:, gw : 2 * gw]
                v = qkv[:, 2 * gw :]
                k_out[at : at + rows, :] = k
                qT_out[:, at : at + rows] = q.T
                vT_out[:, at : at + rows] = v.T
                kT = k.T
                scaled = q.astype(F32) * scale
                hi = scaled.astype(BF16)
                lo = (scaled - hi.astype(F32)).astype(BF16)
                ones = jnp.ones((rows, HD), BF16)
                for h in range(heads):
                    c = slice(h * HD, (h + 1) * HD)
                    qe[h, at : at + rows, 0:128] = jnp.concatenate([hi[:, c], lo[:, c]], axis=1)
                    ke[h, 0:HD, at : at + rows] = kT[c, :]
                    ke[h, HD : 2 * HD, at : at + rows] = kT[c, :]
                    ve[h, at : at + rows, :] = jnp.concatenate([v[:, c], ones], axis=1)

    s = pl.program_id(0)
    parts = []
    for half in range(2):
        inverse = []
        at = pl.multiple_of((s * 2 + half) * rows, rows)
        for h in range(heads):
            scores = mm(qe[h, pl.ds(at, rows), :], ke[h])
            top = jnp.max(scores, axis=1, keepdims=True)
            e = jnp.exp2(scores - top).astype(BF16)
            e_ref[h, half * rows : (half + 1) * rows, :] = e
            o = mm(e, ve[h])
            inv = 1.0 / o[:, HD:]
            inverse.append(inv)
            parts.append((o[:, :HD] * inv).astype(BF16))
        linv_ref[0, half] = jnp.concatenate(inverse, axis=1)
    ctx_ref[0] = jnp.concatenate(parts, axis=1)


def attend(length, x, w, b):
    sources, rows, _ = x.shape
    gw = w.shape[0]
    heads = gw // HD
    slot = sources * 2 * rows
    whole = lambda *shape: pl.BlockSpec(shape, lambda s: (0,) * len(shape))
    return pl.pallas_call(
        attend_kernel,
        grid=(sources,),
        in_specs=[
            pl.BlockSpec(memory_space=pltpu.SMEM),
            whole(*x.shape),
            whole(*w.shape),
            whole(*b.shape),
        ],
        out_specs=[
            pl.BlockSpec((1, rows, 2 * gw), lambda s: (s, 0, 0)),
            pl.BlockSpec((1, 2, rows, gw), lambda s: (s, 0, 0, 0)),
            pl.BlockSpec((heads, 2 * rows, slot), lambda s: (0, s, 0)),
            whole(slot, gw),
            whole(gw, slot),
            whole(gw, slot),
        ],
        out_shape=[
            jax.ShapeDtypeStruct((sources, rows, 2 * gw), BF16),
            jax.ShapeDtypeStruct((sources, 2, rows, gw), F32),
            jax.ShapeDtypeStruct((heads, slot, slot), BF16),
            jax.ShapeDtypeStruct((slot, gw), BF16),
            jax.ShapeDtypeStruct((gw, slot), BF16),
            jax.ShapeDtypeStruct((gw, slot), BF16),
        ],
        scratch_shapes=[
            pltpu.VMEM((heads, slot, 256), BF16),
            pltpu.VMEM((heads, 256, slot), BF16),
            pltpu.VMEM((heads, slot, 128), BF16),
        ],
        compiler_params=pltpu.CompilerParams(vmem_limit_bytes=60 << 20),
        name="attend",
    )(length, x, w, b)


def revisit_kernel(
    e_ref, gctx_ref, ctx_ref, linv_ref, qT_ref, vT_ref, k_ref, x_ref, w_ref,
    gi_ref, gw_ref, gb_ref, vTe, kn, dkT, dvT, gT,
):
    heads = kn.shape[0]
    sources, rows, _ = x_ref.shape
    gw = heads * HD
    slot = sources * 2 * rows
    s = pl.program_id(0)

    @pl.when(s == 0)
    def _():
        dkT[...] = jnp.zeros_like(dkT)
        dvT[...] = jnp.zeros_like(dvT)
        row = lax.broadcasted_iota(jnp.int32, (HD, slot), 0)
        ones_rows = jnp.where(row < 2, 1.0, 0.0).astype(BF16)
        for h in range(heads):
            c = slice(h * HD, (h + 1) * HD)
            vTe[h, 0:HD, :] = vT_ref[c, :]
            vTe[h, HD:, :] = ones_rows
            kn[h] = k_ref[:, c]

    lane = lax.broadcasted_iota(jnp.int32, (rows, HD), 1)
    for half in range(2):
        at = pl.multiple_of((s * 2 + half) * rows, rows)
        lanes = slice(half * gw, (half + 1) * gw)
        g = gctx_ref[0, :, lanes].astype(F32) * linv_ref[0, half]
        g_low = g.astype(BF16)
        gT_low = g_low.T
        prod = g * ctx_ref[0, :, lanes].astype(F32)
        dqs = []
        for h in range(heads):
            c = slice(h * HD, (h + 1) * HD)
            delta = -jnp.sum(prod[:, c], axis=1, keepdims=True)
            d_hi = delta.astype(BF16)
            d_lo = (delta - d_hi.astype(F32)).astype(BF16)
            tail = jnp.where(lane == 0, d_hi, jnp.where(lane == 1, d_lo, jnp.zeros((), BF16)))
            ge = jnp.concatenate([g_low[:, c], tail], axis=1)
            e = e_ref[h, half * rows : (half + 1) * rows, :]
            ds = (e.astype(F32) * mm(ge, vTe[h])).astype(BF16)
            dvT[c, :] += mm(gT_low[c, :], e)
            dkT[c, :] += mm(qT_ref[c, half * rows : (half + 1) * rows], ds)
            dqs.append((mm(ds, kn[h]) * (HD ** (-0.5))).astype(BF16))
        gT[0:gw, pl.ds(at, rows)] = jnp.concatenate(dqs, axis=1).T

    @pl.when(s == sources - 1)
    def _():
        gT[gw : 2 * gw, :] = (dkT[...] * (HD ** (-0.5))).astype(BF16)
        gT[2 * gw :, :] = dvT[...].astype(BF16)
        gb_ref[...] = mm_nt(jnp.ones((8, slot), BF16), gT[...])
        sums = [None, None]
        for t in range(sources):
            packed = []
            for half in range(2):
                cols = slice((t * 2 + half) * rows, (t * 2 + half + 1) * rows)
                part = mm(gT[:, cols], x_ref[t, :, window(half)])
                sums[half] = part if sums[half] is None else sums[half] + part
                packed.append(mm(w_ref[...], gT[:, cols]).T.astype(BF16))
            gi_ref[t] = jnp.concatenate(packed, axis=1)
        gw_ref[...] = (sums[0][:, :gw] + sums[1][:, 64:]).T


def revisit(e, gctx, ctx, linv, qT, vT, k, x, w):
    sources, rows, _ = x.shape
    gw = w.shape[0]
    heads = gw // HD
    slot = sources * 2 * rows
    whole = lambda *shape: pl.BlockSpec(shape, lambda s: (0,) * len(shape))
    return pl.pallas_call(
        revisit_kernel,
        grid=(sources,),
        in_specs=[
            pl.BlockSpec((heads, 2 * rows, slot), lambda s: (0, s, 0)),
            pl.BlockSpec((1, rows, 2 * gw), lambda s: (s, 0, 0)),
            pl.BlockSpec((1, rows, 2 * gw), lambda s: (s, 0, 0)),
            pl.BlockSpec((1, 2, rows, gw), lambda s: (s, 0, 0, 0)),
            pl.BlockSpec((gw, 2 * rows), lambda s: (0, s)),
            whole(*vT.shape),
            whole(*k.shape),
            whole(*x.shape),
            whole(*w.shape),
        ],
        out_specs=[whole(*x.shape), whole(gw, 3 * gw), whole(8, 3 * gw)],
        out_shape=[
            jax.ShapeDtypeStruct(x.shape, BF16),
            jax.ShapeDtypeStruct((gw, 3 * gw), F32),
            jax.ShapeDtypeStruct((8, 3 * gw), F32),
        ],
        scratch_shapes=[
            pltpu.VMEM((heads, 2 * HD, slot), BF16),
            pltpu.VMEM((heads, slot, HD), BF16),
            pltpu.VMEM((gw, slot), F32),
            pltpu.VMEM((gw, slot), F32),
            pltpu.VMEM((3 * gw, slot), BF16),
        ],
        compiler_params=pltpu.CompilerParams(vmem_limit_bytes=60 << 20),
        name="revisit",
    )(e, gctx, ctx, linv, qT, vT, k, x, w)


def split_rows(values):
    mean = jnp.mean(values, axis=-1, keepdims=True)
    centred = values - mean
    var = jnp.mean(centred * centred, axis=-1, keepdims=True)
    return centred, lax.rsqrt(var + epsilon)


def norm_back(grad, unit, inverse, gain):
    g = grad * gain
    m1 = jnp.mean(g, axis=-1, keepdims=True)
    m2 = jnp.mean(g * unit, axis=-1, keepdims=True)
    return inverse * (g - m1 - unit * m2)


def join_windows(parts):
    tiles = []
    for even, odd in zip(parts[0::2], parts[1::2]):
        tiles += [even[:, :128], even[:, 128:] + odd[:, :128], odd[:, 128:]]
    return jnp.concatenate(tiles, axis=1)


def group_window(g):
    at = (g // 2) * 384 + (g % 2) * 128
    return slice(at, at + 256)


def middle_kernel(
    pos_ref, ctx_ref, tok_ref, gout_ref, wo_ref, wu_ref, wd_ref, vec_ref, ub_ref,
    out_ref, gctx_ref, gres_ref, gwo_ref, gwu_ref, gwd_ref, small_ref, upad, dpad, gelu_low,
):
    rows = ctx_ref.shape[1]
    gw = ctx_ref.shape[2] // 2
    width = tok_ref.shape[1]
    hidden = wu_ref.shape[1]
    obias, gain1, shift1, dbias, gain2, shift2 = (vec_ref[i : i + 1, :].astype(F32) for i in range(6))
    for g in range(GROUPS):
        upad[g] = pad_rows(wu_ref[g * gw : (g + 1) * gw, :], g % 2)
        dpad[g] = pad_lanes(wd_ref[g * hidden : (g + 1) * hidden, :], g % 2)
    packed = [[] for _ in range(GROUPS)]
    for half in range(2):
        first = half == 0

        def keep(ref, at, value):
            if first:
                ref[at] = value
            else:
                ref[at] += value

        r = slice(half * rows, (half + 1) * rows)
        x = tok_ref[r, :].astype(F32) + obias
        for g in range(GROUPS):
            x += mm(ctx_ref[g, :, window(half)], pad_rows(wo_ref[g * gw : (g + 1) * gw, :], half))
        c1, i1 = split_rows(x)
        n1 = c1 * i1
        mixed = n1 * gain1 + shift1
        low = mixed.astype(BF16)
        lowered = []
        slopes = []
        actives = []
        for g in range(GROUPS):
            u = mm(low[:, group_window(g)], upad[g]) + ub_ref[g : g + 1, :].astype(F32)
            phi = 0.5 + 0.5 * lax.erf(u * (0.5 ** 0.5))
            slope = phi + u * (jnp.exp(u * u * -0.5) * 0.3989422804014327)
            act = (u * phi).astype(BF16)
            actives.append(act)
            slopes.append(slope)
            lowered.append(mm(act, dpad[g]))
        x = mixed + join_windows(lowered) + dbias
        c2, i2 = split_rows(x)
        n2 = c2 * i2
        row = lax.broadcasted_iota(jnp.int32, (rows, 1), 0) + (pos_ref[1] + half * rows)
        valid = jnp.where(row < pos_ref[0], 1.0, 0.0)
        out_ref[r, :] = (valid * (n2 * gain2 + shift2)).astype(BF16)
        gy = gout_ref[r, :].astype(F32) * valid
        d2 = norm_back(gy, n2, i2, gain2)
        keep(small_ref, slice(4, 5), jnp.sum(gy * n2, axis=0, keepdims=True))
        keep(small_ref, slice(5, 6), jnp.sum(gy, axis=0, keepdims=True))
        keep(small_ref, slice(3, 4), jnp.sum(d2, axis=0, keepdims=True))
        d2_low = d2.astype(BF16)
        backs = []
        for g in range(GROUPS):
            win = d2_low[:, group_window(g)]
            keep(gwd_ref, g, mm_tn(actives[g], win))
            gu = mm_nt(win, dpad[g]) * slopes[g]
            keep(small_ref, slice(6 + g, 7 + g), jnp.sum(gu, axis=0, keepdims=True))
            gu_low = gu.astype(BF16)
            keep(gwu_ref, g, mm_tn(low[:, group_window(g)], gu_low))
            backs.append(mm_nt(gu_low, upad[g]))
        gm = join_windows(backs) + d2
        d1 = norm_back(gm, n1, i1, gain1)
        keep(small_ref, slice(1, 2), jnp.sum(gm * n1, axis=0, keepdims=True))
        keep(small_ref, slice(2, 3), jnp.sum(gm, axis=0, keepdims=True))
        keep(small_ref, slice(0, 1), jnp.sum(d1, axis=0, keepdims=True))
        gres_ref[r, :] = d1
        d1_low = d1.astype(BF16)
        for g in range(GROUPS):
            part = mm_tn(ctx_ref[g, :, window(half)], d1_low)
            keep(gwo_ref, slice(g * gw, (g + 1) * gw), part[64 * half : 64 * half + gw])
        back = mm_nt(d1_low, wo_ref[...]).astype(BF16)
        for g in range(GROUPS):
            packed[g].append(back[:, g * gw : (g + 1) * gw])
    small_ref[10:16, :] = jnp.zeros((6, width), F32)
    for g in range(GROUPS):
        gctx_ref[g] = jnp.concatenate(packed[g], axis=1)


def middle(pos, ctx, tok, gout, wo, wu, wd, vec, ub):
    hidden = wu.shape[1]
    width = tok.shape[1]
    vmem = pl.BlockSpec(memory_space=pltpu.VMEM)
    return pl.pallas_call(
        middle_kernel,
        in_specs=[pl.BlockSpec(memory_space=pltpu.SMEM)] + [vmem] * 8,
        out_specs=[vmem] * 7,
        out_shape=[
            jax.ShapeDtypeStruct(tok.shape, BF16),
            jax.ShapeDtypeStruct(ctx.shape, BF16),
            jax.ShapeDtypeStruct(tok.shape, F32),
            jax.ShapeDtypeStruct(wo.shape, F32),
            jax.ShapeDtypeStruct((GROUPS, 256, hidden), F32),
            jax.ShapeDtypeStruct((GROUPS, hidden, 256), F32),
            jax.ShapeDtypeStruct((16, width), F32),
        ],
        scratch_shapes=[
            pltpu.VMEM((GROUPS, 256, hidden), BF16),
            pltpu.VMEM((GROUPS, hidden, 256), BF16),
            pltpu.VMEM((8, 128), F32),
        ],
        compiler_params=pltpu.CompilerParams(vmem_limit_bytes=62 << 20),
        name="middle",
    )(pos, ctx, tok, gout, wo, wu, wd, vec, ub)


def on_device(
    tokens, lengths, qkv_weight, qv_bias, out_weight, out_bias, norm_gain, norm_shift,
    up_weight, up_bias, down_weight, down_bias, final_gain, final_shift, grad_output,
):
    _, piece_rows, width = tokens.shape
    gw = width // GROUPS
    half = piece_rows // 2
    hidden = up_weight.shape[1]
    me = lax.axis_index("seq")
    gather = lambda a: lax.all_gather(a, "dp", axis=0, tiled=True)
    qkv_full, qv_full = gather(qkv_weight), gather(qv_bias)
    wo, wu, wd = gather(out_weight), gather(up_weight), gather(down_weight)
    vec = jnp.stack([gather(a) for a in (out_bias, norm_gain, norm_shift, down_bias, final_gain, final_shift)])
    vec = jnp.concatenate([vec, jnp.zeros((2, width), BF16)])
    ub = gather(up_bias).reshape(GROUPS, hidden)
    w = lax.dynamic_slice_in_dim(qkv_full, me * gw, gw, 0)
    bias = qv_full.astype(F32).reshape(2, GROUPS, gw)
    bias = lax.dynamic_index_in_dim(bias, me, 1, keepdims=False)
    b = jnp.concatenate([bias[0], jnp.zeros((gw,), F32), bias[1]])[None, :]

    def pack(t):
        return t.reshape(2, half, GROUPS, gw).transpose(2, 1, 0, 3).reshape(GROUPS, half, 2 * gw)

    def unpack(t):
        return t.reshape(GROUPS, half, 2, gw).transpose(2, 1, 0, 3).reshape(piece_rows, width)

    def swap(t):
        return lax.all_to_all(t, "seq", split_axis=0, concat_axis=0, tiled=True)

    x = swap(pack(tokens))
    ctx, linv, e, k, qT, vT = attend(lengths, x, w, b)
    pos = jnp.stack([lengths[0], (me * piece_rows).astype(jnp.int32)])
    ctx_pos = swap(ctx)
    output, gctx, gres, gwo, gwu, gwd, small = middle(
        pos, ctx_pos, tokens[0], grad_output[0], wo, wu, wd, vec, ub
    )
    gi, gwt, gb = revisit(e, swap(gctx), ctx, linv, qT, vT, k, x, w)
    grad_tokens = (unpack(swap(gi)).astype(F32) + gres).astype(BF16)[None]
    gwu = jnp.concatenate([gwu[g, 64 * (g % 2) : 64 * (g % 2) + gw] for g in range(GROUPS)], axis=0)
    gwd = jnp.concatenate([gwd[g, :, 64 * (g % 2) : 64 * (g % 2) + gw] for g in range(GROUPS)], axis=0)
    gqkv = lax.dynamic_update_slice_in_dim(jnp.zeros((width, 3 * gw), F32), gwt, me * gw, 0)
    gqv = jnp.zeros((2, GROUPS, gw), F32)
    gqv = lax.dynamic_update_slice(gqv, jnp.stack([gb[0, :gw], gb[0, 2 * gw :]])[:, None], (0, me, 0))

    def total(a):
        return lax.psum(lax.psum_scatter(a, "dp", scatter_dimension=0, tiled=True), "seq")

    return (
        output[None], grad_tokens, total(gqkv), total(gqv.reshape(-1)), total(gwo), total(small[0]),
        total(small[1]), total(small[2]), total(gwu), total(small[6:10].reshape(-1)), total(gwd),
        total(small[3]), total(small[4]), total(small[5]),
    )


def solution(mesh):
    rows = P("dp", "seq", None)
    mat = P("dp", None)
    vec = P("dp")
    in_specs = (rows, vec, mat, vec, mat, vec, vec, vec, mat, vec, mat, vec, vec, vec, rows)
    out_specs = (rows, rows, mat, vec, mat, vec, vec, vec, mat, vec, mat, vec, vec, vec)
    return jax.shard_map(on_device, mesh=mesh, in_specs=in_specs, out_specs=out_specs, check_vma=False)
```

time: 660 us -> 586 us (0.89)
  waiting for transfers between devices: 89.1 us -> 273 us
  matrix products: 161 us -> 0 us
  other arithmetic: 87.8 us -> 7.06 us
  Pallas kernels: 0 us -> 76.8 us
  local copies, waits for them, and re-layouts: 79 us -> 32.5 us
  blocking collectives: 193 us -> 157 us
  loops' own time: 13.4 us -> 0 us
    reduce_scatter x4, waiting for transfers between devices: 52 us -> 271 us  [total(): lax.psum_scatter(a, 'dp', scatter_dimension=0, tiled=True)]
    dot_general x40 -> x0, matrix products: 161 us -> none  [the longest x3 23.4 us: group_mult(): jnp.einsum('ngi,gio->ngo', values, matrix, preferred_element_type=jnp.flo...]
    pallas_call x0 -> x3, Pallas kernels: none -> 76.8 us  [the longest x1 31.3 us: revisit(): pl.pallas_call(revisit_kernel, grid=(sources,), in_specs=[pl.BlockSpec((h...]
    convert_element_type x31 -> x0, other arithmetic: 41.9 us -> none  [the longest x4 19.9 us: revisit_block(): grad_scores = (probs * (grad_probs - inner_sum)).astype(jnp.bfloat16)]
    all_to_all x1, blocking collectives: 53.8 us -> 15.9 us  [swap(): return lax.all_to_all(t, 'seq', split_axis=0, concat_axis=0, tiled=True)]
    all_to_all x3, waiting for transfers between devices: 35.3 us -> 0.01 us  [swap(): return lax.all_to_all(t, 'seq', split_axis=0, concat_axis=0, tiled=True)]
    reduce_sum x14 -> x0, other arithmetic: 26.5 us -> none  [the longest x4 11.2 us: attend_block(): row_total = jnp.sum(exponent, axis=-1, keepdims=True)]
    reshape x8 -> x6, local copies, waits for them, and re-layouts: 21.2 us -> 2.12 us  [the longest x2 1.34 us: pack(): t.reshape(2, half, GROUPS, gw).transpose(2, 1, 0, 3)]
  transfers between devices with their start and end apart: 11 -> 11, of which waited for: 3 -> 4; matrix products, arithmetic and copies ran while one was open for 45% -> 4% of each run, Pallas kernels for 0% -> 5%
where the time goes in v1:
time: 586 us; the launch traced here: 577 us
  waiting for transfers between devices  273 us (47%)
  blocking collectives  157 us (27%)
  Pallas kernels  76.8 us (13%)
  local copies, waits for them, and re-layouts  32.5 us (6%)
  between operations  18.8 us (3%)
  starting transfers between devices  11.6 us (2%)
  other arithmetic  7.06 us (1%)
    reduce_scatter x4, waiting for transfers between devices, total(): lax.psum_scatter(a, 'dp', scatter_dimension=0, tiled=True)  271 us
    unnamed x2, blocking collectives  74 us
    all_gather x2, blocking collectives, on_device(): gather = lambda a: lax.all_gather(a, 'dp', axis=0, tiled=True)  60.9 us
    pallas_call x1, Pallas kernels, revisit(): pl.pallas_call(revisit_kernel, grid=(sources,), in_specs=[pl.BlockSpec((h...  31.3 us
    pallas_call x1, Pallas kernels, attend(): pl.pallas_call(attend_kernel, grid=(sources,), in_specs=[pl.BlockSpec(mem...  26.6 us
    pallas_call x1, Pallas kernels, middle(): pl.pallas_call(middle_kernel, in_specs=[pl.BlockSpec(memory_space=pltpu.S...  18.9 us
    unnamed x60, local copies, waits for them, and re-layouts  17.8 us
    all_to_all x1, blocking collectives, swap(): return lax.all_to_all(t, 'seq', split_axis=0, concat_axis=0, tiled=True)  15.9 us
  transfers between devices with their start and end apart: 11, of which 4 were waited for; matrix products, arithmetic and copies ran while one was open for 4% of the time, Pallas kernels for 5%

profile of v1, /device:TPU:0, one launch (start us, length us, event | category | flops | bytes accessed | tf_op | source)
XLA Modules:
  0.0 577.2 jit_solution(12464993512233607277)
XLA Ops:
  7.2 1.7 copy.54
  9.0 0.7 all-gather.5.cloned.1.call-update
  9.8 0.7 all-gather.7.cloned.1.call-update
  10.5 1.4 copy.51
  12.3 1.2 copy.53
  13.4 4.2 all-to-all-start
  17.7 0.6 fusion.2
  19.6 0.2 dynamic-update-slice.1
  20.5 0.2 dynamic-update-slice.5
  21.0 0.2 dynamic-update-slice
  21.3 38.7 %all-reduce.18 = (bf16[1536]{0:T(1024)(128)(2,1)S(1)}, bf16[768]{0:T(1024)(128)(2,1)S(1)}, bf16[768]{0:T(1024)(128)(2,1)S(1)}, bf16[768]{0:T(1024)(128)(2,1)S(1)...) all-reduce(bf16[1536]{0:T(1024)(128)(2,1)S(1)} %dynamic-update-slic, ...), channel_id=1, replica_groups=mesh['dp'=8,'seq'=4] {'dp'}, use_global_device_ids=true, to_apply=%add | all-reduce | flops 6144 | bytes 24576
  60.1 0.6 broadcast_in_dim.25.b_ref
  61.4 34.5 %all_gather.36 = bf16[768,576]{1,0:T(8,128)(2,1)S(1)} all-gather(bf16[96,576]{1,0:T(8,128)(2,1)S(1)} %copy-done.4), channel_id=1, replica_groups=mesh['dp'=8,'seq'=4] {'dp'}, dimensions={0}, use_global_device_ids=true | all-gather | bytes 995328 | tf_op jit(solution)/shard_map/all_gather | solution.py:387
  95.9 0.7 constant_dynamic-slice_fusion.2.w_ref
  96.6 0.9 copy-done.1
  97.5 26.6 %attend.1 = (bf16[4,256,384]{2,1,0:T(8,128)(2,1)}, f32[4,2,256,192]{3,2,1,0:T(8,128)}, bf16[3,2048,2048]{2,1,0:T(8,128)(2,1)}, bf16[2048,192]{1,0:T(8,128)(2,1)}...) custom-call(s32[1]{0:T(128)S(6)} %copy.75.len_ref, bf16[4,256,384]{2,1,0:T(8,128)(2,1)} %copy-done.1, ...), custom_call_target="tpu_custom_call" | custom-call | tf_op jit(solution)/shard_map/attend/pallas_call | solution.py:110
  124.1 3.5 all-to-all-start.1
  127.7 26.3 %all-gather = bf16[8,1,384]{2,1,0:T(2,128)(2,1)S(1)} all-gather(bf16[1,1,384]{2,1,0:T(2,128)(2,1)S(1)} %reshape.91), channel_id=1, replica_groups=mesh['dp'=8,'seq'=4] {'dp'}, dimensions={0}, use_global_device_ids=true | all-gather | bytes 6912 | tf_op jit(solution)/shard_map/all_gather | solution.py:387
  154.1 0.6 reshape.63.ub_ref
  154.7 0.6 concatenate.13.vec_ref
  155.4 0.6 pad_add_fusion.pos_ref
  156.0 0.8 copy-done.2
  156.9 18.9 %middle.1 = (bf16[512,768]{1,0:T(8,128)(2,1)}, bf16[4,256,384]{2,1,0:T(8,128)(2,1)}, f32[512,768]{1,0:T(8,128)}, f32[768,768]{1,0:T(8,128)}, f32[4,256,768]{2,1,...) custom-call(s32[2]{0:T(128)} %pad_add_fusion.pos_ref, bf16[4,256,384]{2,1,0:T(8,128)(2,1)} %copy-done.2, ...), custom_call_target="tpu_custom_call" | custom-call | tf_op jit(solution)/shard_map/middle/pallas_call | solution.py:355
  175.8 15.9 %all_to_all.20.gctx_ref = bf16[4,256,384]{2,1,0:T(8,128)(2,1)} all-to-all(bf16[4,256,384]{2,1,0:T(8,128)(2,1)} %get-tuple-element.33), channel_id=1, replica_groups=mesh['dp'=8,'seq'=4] {'seq'}, dimensions={0} | all-to-all | bytes 1572864 | tf_op jit(solution)/shard_map/all_to_all | solution.py:405
  191.7 31.3 %revisit.1 = (bf16[4,256,384]{2,1,0:T(8,128)(2,1)}, f32[192,576]{1,0:T(8,128)}, f32[8,576]{1,0:T(8,128)}) custom-call(bf16[3,2048,2048]{2,1,0:T(8,128)(2,1)} %get-tuple-element.32.e_ref, bf16[4,256,384]{2,1,0:T(8,128)(2,1)} %all_to_all.20.gctx_ref, bf16[4,256,384]{2,1,0:T(8,128)(2,1)} %get-tuple-element.30.ctx_ref, ...), custom_call_target="tpu_custom_call" | custom-call | tf_op jit(solution)/shard_map/revisit/pallas_call | solution.py:213
  223.1 1.1 constant_dynamic-update-slice_fusion
  224.2 1.3 copy-done
  225.6 2.3 slice_bitcast_fusion.3
  227.9 1.8 pad_maximum_fusion
  229.9 1.8 copy-done.3
  231.8 1.6 pad_maximum_fusion.1
  233.5 0.7 reduce-scatter.7.cloned.1.call-update
  234.2 3.5 all-to-all-start.3
  239.8 49.6 %reduce-scatter.5.cloned.1.call-done = f32[96,576]{1,0:T(8,128)} async-done(((f32[768,576]{1,0:T(8,128)}), f32[96,576]{1,0:T(8,128)}) %reduce-scatter.5.cloned.1.call-update) | async-done | bytes 221200 | tf_op jit(solution)/shard_map/reduce_scatter | solution.py:423
  289.5 76.8 %reduce-scatter.11.cloned.1.call-done = f32[384,192]{1,0:T(8,128)} async-done(((f32[3072,192]{1,0:T(8,128)}), f32[384,192]{1,0:T(8,128)}) %reduce-scatter.11.cloned.1.call-update) | async-done | bytes 294928 | tf_op jit(solution)/shard_map/reduce_scatter | solution.py:423
  366.2 72.1 %reduce-scatter.9.cloned.1.call-done = f32[96,768]{1,0:T(8,128)} async-done(((f32[768,768]{1,0:T(8,128)}), f32[96,768]{1,0:T(8,128)}) %reduce-scatter.9.cloned.1.call-update) | async-done | bytes 294928 | tf_op jit(solution)/shard_map/reduce_scatter | solution.py:423
  438.3 72.3 %reduce-scatter.7.cloned.1.call-done = f32[96,768]{1,0:T(8,128)} async-done(((f32[768,768]{1,0:T(8,128)}), f32[96,768]{1,0:T(8,128)}) %reduce-scatter.7.cloned.1.call-update) | async-done | bytes 294928 | tf_op jit(solution)/shard_map/reduce_scatter | solution.py:423
  510.7 0.7 fusion.1
  511.6 35.4 %all-reduce.15 = (f32[1536]{0:T(1024)S(1)}, f32[768]{0:T(1024)S(1)}, f32[768]{0:T(1024)S(1)}, f32[768]{0:T(1024)S(1)}, f32[3072]{0:T(1024)S(1)}, /*index=5*/f32[...) all-reduce(f32[1536]{0:T(1024)S(1)} %reshape.64, ...), channel_id=3, replica_groups=mesh['dp'=8,'seq'=4] {'dp'}, use_global_device_ids=true, to_apply=%region_2.3.clone | all-reduce | flops 9216 | bytes 73728
  547.5 6.6 %all-reduce.16 = (f32[192]{0:T(256)}, f32[96]{0:T(128)}, f32[96]{0:T(128)}, f32[96]{0:T(128)}, f32[384]{0:T(512)}, /*index=5*/f32[96]{0:T(128)}, f32[96]{0:T(128)}, f32[96]{0:T(128)}) all-reduce(f32[192]{0:T(256)S(1)} %dynamic-slice.8, f32[96]{0:T(128)S(1)} %dynamic-slice.10, ...), channel_id=1, replica_groups=mesh['dp'=8,'seq'=4] {'seq'}, use_global_device_ids=true, to_apply=%region_3.4 | all-reduce | flops 1152 | bytes 9216 | tf_op jit(solution)/shard_map/psum | solution.py:423
  554.1 1.5 copy.55
  555.5 2.0 copy.60
  557.5 2.5 reshape.116
  560.1 2.9 fusion
  563.0 1.9 copy.59
  564.8 1.7 copy.76
  566.5 1.7 copy.77
  568.2 1.7 copy.78
  (90 shorter events, 3.1 us)
Async XLA Ops:
  7.2 148.8 %all-gather.9.cloned.1.call-start = ((), (), s32[]{:S(2)}) async-start(), calls=%async_computation.10 | async-start | bytes 1769472 | tf_op jit(solution)/shard_map/all_gather | solution.py:387
  9.0 147.0 %all-gather.5.cloned.1.call-start = ((), (), s32[]{:S(2)}) async-start(), calls=%async_computation.8 | async-start | bytes 1327104 | tf_op jit(solution)/shard_map/all_gather | solution.py:387
  9.7 146.3 %all-gather.7.cloned.1.call-start = ((), (), s32[]{:S(2)}) async-start(), calls=%async_computation.9 | async-start | bytes 1327104 | tf_op jit(solution)/shard_map/all_gather | solution.py:387
  12.1 5.6 copy-start.6
  12.1 7.5 %copy-start.8 = (bf16[96]{0:T(256)(128)(2,1)S(1)}, bf16[96]{0:T(256)(128)(2,1)}, u32[]{:S(2)}) copy-start(bf16[96]{0:T(256)(128)(2,1)} %param.20) | copy-start | bytes 580
  12.1 7.7 %copy-start.9 = (bf16[96]{0:T(256)(128)(2,1)S(1)}, bf16[96]{0:T(256)(128)(2,1)}, u32[]{:S(2)}) copy-start(bf16[96]{0:T(256)(128)(2,1)} %param.21) | copy-start | bytes 580
  12.1 8.0 %copy-start.10 = (bf16[96]{0:T(256)(128)(2,1)S(1)}, bf16[96]{0:T(256)(128)(2,1)}, u32[]{:S(2)}) copy-start(bf16[96]{0:T(256)(128)(2,1)} %param.22) | copy-start | bytes 580
  12.1 8.2 %copy-start.11 = (bf16[96]{0:T(256)(128)(2,1)S(1)}, bf16[96]{0:T(256)(128)(2,1)}, u32[]{:S(2)}) copy-start(bf16[96]{0:T(256)(128)(2,1)} %param.26) | copy-start | bytes 580
  12.1 8.4 %copy-start.12 = (bf16[96]{0:T(256)(128)(2,1)S(1)}, bf16[96]{0:T(256)(128)(2,1)}, u32[]{:S(2)}) copy-start(bf16[96]{0:T(256)(128)(2,1)} %param.27) | copy-start | bytes 580
  12.1 8.6 %copy-start.13 = (bf16[96]{0:T(256)(128)(2,1)S(1)}, bf16[96]{0:T(256)(128)(2,1)}, u32[]{:S(2)}) copy-start(bf16[96]{0:T(256)(128)(2,1)} %param.28) | copy-start | bytes 580
  12.2 8.9 %copy-start.14 = (bf16[192]{0:T(256)(128)(2,1)S(1)}, bf16[192]{0:T(256)(128)(2,1)}, u32[]{:S(2)}) copy-start(bf16[192]{0:T(256)(128)(2,1)} %param.18) | copy-start | bytes 1156
  12.2 49.2 %copy-start.4 = (bf16[96,576]{1,0:T(8,128)(2,1)S(1)}, bf16[96,576]{1,0:T(8,128)(2,1)}, u32[]{:S(2)}) copy-start(bf16[96,576]{1,0:T(8,128)(2,1)} %param.17) | copy-start | bytes 331780
  13.4 83.2 %all-to-all-start = ((bf16[4,256,384]{2,1,0:T(8,128)(2,1)}), bf16[4,256,384]{2,1,0:T(8,128)(2,1)S(1)}, u32[]{:S(2)}, u32[]{:S(2)}) async-start(bf16[4,256,384]{2,1,0:T(8,128)(2,1)} %copy.53), calls=%async_computation | async-start | bytes 1572864 | tf_op jit(solution)/shard_map/all_to_all | solution.py:405
  17.7 110.0 %copy-start.7 = (bf16[384]{0:T(512)(128)(2,1)S(1)}, bf16[384]{0:T(512)(128)(2,1)}, u32[]{:S(2)}) copy-start(bf16[384]{0:T(512)(128)(2,1)} %param.24) | copy-start | bytes 2308
  96.6 0.9 copy-start.1
  124.1 31.9 %all-to-all-start.1 = ((bf16[4,256,384]{2,1,0:T(8,128)(2,1)}), bf16[4,256,384]{2,1,0:T(8,128)(2,1)S(1)}, u32[]{:S(2)}, u32[]{:S(2)}) async-start(bf16[4,256,384]{2,1,0:T(8,128)(2,1)} %get-tuple-element.30.ctx_ref), calls=%async_computation.1 | async-start | bytes 1572864 | tf_op jit(solution)/shard_map/all_to_all | solution.py:405
  127.6 161.9 %reduce-scatter.5.cloned.1.call-start = ((), (), s32[]{:S(2)}) async-start(), calls=%async_computation.11 | async-start | bytes 2211840 | tf_op jit(solution)/shard_map/reduce_scatter | solution.py:423
  156.0 0.9 copy-start.2
  224.2 1.3 copy-start
  225.5 140.7 %reduce-scatter.11.cloned.1.call-start = ((), (), s32[]{:S(2)}) async-start(), calls=%async_computation.14 | async-start | bytes 3538944 | tf_op jit(solution)/shard_map/reduce_scatter | solution.py:423
  229.8 1.9 copy-start.3
  229.8 208.5 %reduce-scatter.9.cloned.1.call-start = ((), (), s32[]{:S(2)}) async-start(), calls=%async_computation.13 | async-start | bytes 2654208 | tf_op jit(solution)/shard_map/reduce_scatter | solution.py:423
  233.5 6.3 %copy-start.5 = (f32[16,768]{1,0:T(8,128)S(1)}, f32[16,768]{1,0:T(8,128)}, u32[]{:S(2)}) copy-start(f32[16,768]{1,0:T(8,128)} %get-tuple-element.43) | copy-start | bytes 147460
  233.5 277.2 %reduce-scatter.7.cloned.1.call-start = ((), (), s32[]{:S(2)}) async-start(), calls=%async_computation.12 | async-start | bytes 2654208 | tf_op jit(solution)/shard_map/reduce_scatter | solution.py:423
  234.2 319.9 %all-to-all-start.3 = ((bf16[4,256,384]{2,1,0:T(8,128)(2,1)}), bf16[4,256,384]{2,1,0:T(8,128)(2,1)S(1)}, u32[]{:S(2)}, u32[]{:S(2)}) async-start(bf16[4,256,384]{2,1,0:T(8,128)(2,1)} %get-tuple-element.38), calls=%async_computation.3 | async-start | bytes 1572864 | tf_op jit(solution)/shard_map/all_to_all | solution.py:405
  237.7 325.2 %all-reduce.21.cloned.1.call-start = ((), (), s32[]{:S(2)}) async-start(), calls=%async_computation.15 | async-start | bytes 2457600 | tf_op jit(solution)/shard_map/psum | solution.py:423
Sparse Core Ops, SparseCore 0:
  10.7 47.7 all-gather.8
  60.7 43.0 all-gather.4
  106.0 40.0 all-gather.6
  225.7 63.7 reduce-scatter.4
  292.9 73.2 reduce-scatter.10
  369.6 68.7 reduce-scatter.8
  441.8 68.7 reduce-scatter.6
  513.3 37.5 all-reduce.20

commit v2 on v1

v2 whole, which is shorter than its diff:
```python
import functools

import jax
import jax.numpy as jnp
from jax import lax
from jax.experimental import pallas as pl
from jax.experimental.pallas import tpu as pltpu
from jax.sharding import PartitionSpec as P

H = 12
GROUPS = 4
HD = 64
epsilon = 1e-05
LOG2E = 1.4426950408889634
MASKED = -1e30
F32 = jnp.float32
BF16 = jnp.bfloat16


def mm(a, b):
    return jnp.dot(a, b, preferred_element_type=F32)


def mm_nt(a, b):
    return lax.dot_general(a, b, (((1,), (1,)), ((), ())), preferred_element_type=F32)


def mm_tn(a, b):
    return lax.dot_general(a, b, (((0,), (0,)), ((), ())), preferred_element_type=F32)


def pad_rows(w, half):
    zeros = jnp.zeros((64, w.shape[1]), w.dtype)
    return jnp.concatenate([w, zeros] if half == 0 else [zeros, w], axis=0)


def pad_lanes(w, half):
    zeros = jnp.zeros((w.shape[0], 64), w.dtype)
    return jnp.concatenate([w, zeros] if half == 0 else [zeros, w], axis=1)


def window(half):
    return slice(half * 128, half * 128 + 256)


MESH = pl.DeviceIdType.MESH


def remote(src, dst, send_sem, recv_sem, dp, seq):
    return pltpu.make_async_remote_copy(
        src_ref=src, dst_ref=dst, send_sem=send_sem, recv_sem=recv_sem,
        device_id={"dp": dp, "seq": seq}, device_id_type=MESH,
    )


def greet(n, group, i, s):
    barrier = pltpu.get_barrier_semaphore()
    for d in range(1, n):
        pl.semaphore_signal(barrier, inc=1, device_id={"dp": lax.rem(i + d, n), "seq": s}, device_id_type=MESH)
    for d in range(1, group):
        pl.semaphore_signal(barrier, inc=1, device_id={"dp": i, "seq": lax.rem(s + d, group)}, device_id_type=MESH)
    pl.semaphore_wait(barrier, n + group - 2)


def other(index):
    return index + 1 - 2 * lax.rem(index, 2)


def half_of(ref, lead, c):
    if len(ref.shape) == len(lead) + 3:
        return ref.at[lead + (c,)]
    lanes = ref.shape[-1] // 2
    at = pl.multiple_of(c * lanes, 128) if lanes % 128 == 0 else c * lanes
    return ref.at[lead + (slice(None), pl.ds(at, lanes))]


def stack_rows(pieces):
    if len(pieces) == 1:
        return pieces[0]
    if pieces[0].shape[0] % 16 == 0:
        return jnp.concatenate(pieces, axis=0)
    return jnp.concatenate([p.astype(F32) for p in pieces], axis=0).astype(pieces[0].dtype)


def join_lanes(pieces):
    return pieces[0] if len(pieces) == 1 else jnp.concatenate(pieces, axis=1)


def attend_kernel(
    n, per, len_ref, x_in, wq_in, vec_in, wo_in, wu_in, wd_in,
    ctx_ref, linv_ref, e_ref, k_out, qT_out, vT_out, w_out, vec_out, x_out, ctx_pos, wo_out, wu_out, wd_out,
    qe, ke, ve, x_buf, ctx_buf, wq_buf, vec_buf,
    x_send, x_recv, c_send, c_recv, q_send, q_recv, v_send, v_recv, z_send, z_recv, y_send, y_recv, p_send, p_recv, own, local,
):
    heads = qe.shape[0]
    sources, rows, _ = x_buf.shape
    gw = heads * HD
    slot = sources * 2 * rows
    parts_q = wq_buf.shape[0]
    t = pl.program_id(0)
    i = lax.axis_index("dp")
    me = lax.axis_index("seq")
    c = lax.rem(me, 2)
    y = lax.rem(i, 2)
    k = i // 2
    depth = n // 2
    weights = ((wo_in, wo_out), (wu_in, wu_out), (wd_in, wd_out))

    def x_copy(d):
        peer = lax.rem(me + d, sources)
        return remote(x_in.at[peer], x_buf.at[sources - 1 - d], x_send.at[d - 1], x_recv.at[d - 1], i, peer)

    def ctx_copy(d):
        peer = lax.rem(me + d, sources)
        return remote(ctx_buf.at[d - 1], ctx_pos.at[me], c_send.at[d - 1], c_recv.at[d - 1], i, peer)

    def q_copy(d):
        piece = jnp.clip(i - me * parts_q, 0, parts_q - 1)
        return remote(wq_in, wq_buf.at[piece], q_send.at[d - 1], q_recv.at[piece], lax.rem(i + d, n), me)

    def v_copy(d):
        return remote(vec_in, vec_buf.at[i], v_send.at[d - 1], v_recv.at[d - 1], lax.rem(i + d, n), me)

    def z_copy(w, d):
        src, dst = weights[w]
        to = lax.rem(k + d, depth)
        return remote(
            half_of(src, (), c), half_of(dst, (k, y), c), z_send.at[w, d - 1], z_recv.at[w, d - 1], to * 2 + y, me
        )

    def own_copy(w):
        src, dst = weights[w]
        return pltpu.make_async_copy(half_of(src, (), c), half_of(dst, (k, y), c), own.at[w])

    def y_copy(w):
        part = half_of(weights[w][1], (slice(None), y), c)
        return remote(part, part, y_send.at[w], y_recv.at[w], other(i), me)

    def p_copy(w):
        part = half_of(weights[w][1], (slice(None), slice(None)), c)
        return remote(part, part, p_send.at[w], p_recv.at[w], i, other(me))

    x_own = pltpu.make_async_copy(x_in.at[me], x_buf.at[sources - 1], local.at[0])
    x_keep = pltpu.make_async_copy(x_buf, x_out, local.at[1])
    v_own = pltpu.make_async_copy(vec_in, vec_buf.at[i], local.at[2])
    ctx_own = pltpu.make_async_copy(ctx_buf.at[sources - 1], ctx_pos.at[me], local.at[3])
    sender = i // parts_q == me

    @pl.when(t == 0)
    def _():
        greet(n, sources, i, me)
        for d in (2, 1, 3):
            x_copy(d).start()
        x_own.start()

        @pl.when(sender)
        def _():
            for d in range(1, n):
                q_copy(d).start()
            pltpu.make_async_copy(wq_in, wq_buf.at[jnp.clip(i - me * parts_q, 0, parts_q - 1)], local.at[4]).start()

        v_own.start()
        for d in range(1, n):
            v_copy(d).start()
        for w in range(3):
            for d in range(1, depth):
                z_copy(w, d).start()
            own_copy(w).start()

        scale = HD ** (-0.5) * LOG2E
        lane = lax.broadcasted_iota(jnp.int32, (slot, 128), 1)
        ones_lane = jnp.where(lane == 0, 1.0, 0.0).astype(BF16)
        key_row = lax.broadcasted_iota(jnp.int32, (128, 2 * rows), 0)
        for h in range(heads):
            qe[h, :, 128:256] = ones_lane
        for j in range(sources):
            first = lax.rem(me + 1 + j, sources) * (2 * rows)
            key_pos = lax.broadcasted_iota(jnp.int32, (128, 2 * rows), 1) + first
            bias = jnp.where((key_row == 0) & (key_pos >= len_ref[0]), MASKED, 0.0).astype(BF16)
            for h in range(heads):
                ke[h, 128:256, j * 2 * rows : (j + 1) * 2 * rows] = bias

        for piece in range(parts_q):
            @pl.when(jnp.logical_not(jnp.logical_and(sender, i - me * parts_q == piece)))
            def _():
                remote(wq_in, wq_buf.at[piece], q_send.at[0], q_recv.at[piece], other(i), me).wait_recv()

        @pl.when(sender)
        def _():
            pltpu.make_async_copy(wq_in, wq_buf.at[jnp.clip(i - me * parts_q, 0, parts_q - 1)], local.at[4]).wait()

        v_own.wait()
        for d in range(1, n):
            v_copy(d).wait_recv()
        vec_out[...] = vec_buf[...]
        count = gw // per
        q_bias = join_lanes([vec_buf[me * count + u, 0:1, 0:per] for u in range(count)])
        v_bias = join_lanes([vec_buf[(GROUPS + me) * count + u, 0:1, 0:per] for u in range(count)])
        b = jnp.concatenate([q_bias, jnp.zeros((1, gw), F32), v_bias], axis=1)
        weight = stack_rows([wq_buf[u] for u in range(parts_q)])
        w_out[...] = weight
        x_own.wait()
        for j in (3, 0, 2, 1):
            if j < sources - 1:
                x_copy(sources - 1 - j).wait_recv()
            for half in range(2):
                at = (j * 2 + half) * rows
                w = pad_rows(weight, half)
                qkv = (mm(x_buf[j, :, window(half)], w) + b).astype(BF16)
                q = qkv[:, :gw]
                kk = qkv[:, gw : 2 * gw]
                v = qkv[:, 2 * gw :]
                k_out[at : at + rows, :] = kk
                qT_out[:, at : at + rows] = q.T
                vT_out[:, at : at + rows] = v.T
                kT = kk.T
                scaled = q.astype(F32) * scale
                hi = scaled.astype(BF16)
                lo = (scaled - hi.astype(F32)).astype(BF16)
                ones = jnp.ones((rows, HD), BF16)
                for h in range(heads):
                    cols = slice(h * HD, (h + 1) * HD)
                    qe[h, at : at + rows, 0:128] = jnp.concatenate([hi[:, cols], lo[:, cols]], axis=1)
                    ke[h, 0:HD, at : at + rows] = kT[cols, :]
                    ke[h, HD : 2 * HD, at : at + rows] = kT[cols, :]
                    ve[h, at : at + rows, :] = jnp.concatenate([v[:, cols], ones], axis=1)
        x_keep.start()

    def step_y(w):
        own_copy(w).wait()
        for d in range(1, depth):
            z_copy(w, d).wait_recv()
        y_copy(w).start()

    def step_p(w):
        y_copy(w).wait_recv()
        p_copy(w).start()

    plan = {
        (0, 0): [(step_y, 0)], (0, 4): [(step_y, 1)], (1, 2): [(step_p, 0)], (1, 4): [(step_y, 2)],
        (2, 3): [(step_p, 1)], (3, 2): [(step_p, 2)],
    }

    parts = []
    for half in range(2):
        inverse = []
        at = pl.multiple_of((t * 2 + half) * rows, rows)
        for h in range(heads):
            for (when_t, point), actions in plan.items():
                if point == half * heads + h:
                    @pl.when(t == when_t)
                    def _(actions=actions):
                        for fn, w in actions:
                            fn(w)
            if half == 0 and h == 1:
                for d in range(1, sources):
                    @pl.when(t == d)
                    def _(d=d):
                        ctx_copy(d).start()
            scores = mm(qe[h, pl.ds(at, rows), :], ke[h])
            top = jnp.max(scores, axis=1, keepdims=True)
            e = jnp.exp2(scores - top).astype(BF16)
            e_ref[h, half * rows : (half + 1) * rows, :] = e
            o = mm(e, ve[h])
            inv = 1.0 / o[:, HD:]
            inverse.append(inv)
            parts.append((o[:, :HD] * inv).astype(BF16))
        linv_ref[0, half] = jnp.concatenate(inverse, axis=1)
    block = jnp.concatenate(parts, axis=1)
    ctx_ref[0] = block
    ctx_buf[t] = block

    @pl.when(t == sources - 1)
    def _():
        ctx_own.start()
        for d in range(1, sources):
            x_copy(d).wait_send()
            ctx_copy(d).wait_send()
            ctx_copy(d).wait_recv()

        @pl.when(sender)
        def _():
            for d in range(1, n):
                q_copy(d).wait_send()

        for d in range(1, n):
            v_copy(d).wait_send()
        for w in range(3):
            for d in range(1, depth):
                z_copy(w, d).wait_send()
            y_copy(w).wait_send()
            p_copy(w).wait()
        x_keep.wait()
        ctx_own.wait()


def attend(n, per, length, x, wq, vec, wo, wu, wd):
    sources, rows, _ = x.shape
    gw = wq.shape[1] // 3
    heads = gw // HD
    slot = sources * 2 * rows
    parts_q = n // GROUPS
    depth = n // 2
    whole = lambda *shape: pl.BlockSpec(shape, lambda s: (0,) * len(shape), pipeline_mode=pl.Buffered(1))
    out_whole = lambda *shape: pl.BlockSpec(shape, lambda s: (0,) * len(shape))
    anywhere = pl.BlockSpec(memory_space=pl.ANY)
    dma = lambda *shape: pltpu.SemaphoreType.DMA(shape)
    return pl.pallas_call(
        functools.partial(attend_kernel, n, per),
        grid=(sources,),
        in_specs=[
            pl.BlockSpec(memory_space=pltpu.SMEM), anywhere, anywhere, whole(*vec.shape),
            whole(*wo.shape), whole(*wu.shape), whole(*wd.shape),
        ],
        out_specs=[
            pl.BlockSpec((1, rows, 2 * gw), lambda s: (s, 0, 0)),
            pl.BlockSpec((1, 2, rows, gw), lambda s: (s, 0, 0, 0)),
            pl.BlockSpec((heads, 2 * rows, slot), lambda s: (0, s, 0)),
            out_whole(slot, gw),
            out_whole(gw, slot),
            out_whole(gw, slot),
            out_whole(gw, 3 * gw),
            out_whole(n, *vec.shape),
            anywhere, anywhere, anywhere, anywhere, anywhere,
        ],
        out_shape=[
            jax.ShapeDtypeStruct((sources, rows, 2 * gw), BF16),
            jax.ShapeDtypeStruct((sources, 2, rows, gw), F32),
            jax.ShapeDtypeStruct((heads, slot, slot), BF16),
            jax.ShapeDtypeStruct((slot, gw), BF16),
            jax.ShapeDtypeStruct((gw, slot), BF16),
            jax.ShapeDtypeStruct((gw, slot), BF16),
            jax.ShapeDtypeStruct((gw, 3 * gw), BF16),
            jax.ShapeDtypeStruct((n,) + vec.shape, F32),
            jax.ShapeDtypeStruct(x.shape, BF16),
            jax.ShapeDtypeStruct(x.shape, BF16),
            jax.ShapeDtypeStruct((depth, 2) + wo.shape, BF16),
            jax.ShapeDtypeStruct((depth, 2) + wu.shape, BF16),
            jax.ShapeDtypeStruct((depth, 2) + wd.shape, BF16),
        ],
        scratch_shapes=[
            pltpu.VMEM((heads, slot, 256), BF16),
            pltpu.VMEM((heads, 256, slot), BF16),
            pltpu.VMEM((heads, slot, 128), BF16),
            pltpu.VMEM(x.shape, BF16),
            pltpu.VMEM(x.shape, BF16),
            pltpu.VMEM((parts_q,) + wq.shape, BF16),
            pltpu.VMEM((n,) + vec.shape, F32),
            dma(3), dma(3), dma(3), dma(3), dma(n - 1), dma(parts_q), dma(n - 1), dma(n - 1),
            dma(3, depth - 1), dma(3, depth - 1), dma(3), dma(3), dma(3), dma(3), dma(3), dma(5),
        ],
        compiler_params=pltpu.CompilerParams(vmem_limit_bytes=60 << 20, collective_id=1, has_side_effects=True),
        name="attend",
    )(length, x, wq, vec, wo, wu, wd)


def revisit_kernel(
    n, per,
    e_ref, ctx_ref, linv_ref, qT_ref, vT_ref, k_ref, x_ref, w_ref, gres_ref, gctx_in, gwo_in, gwu_in, gwd_in, sm_in,
    gt_ref, gqkv_ref, gqv_ref, gwo_ref, gwu_ref, gwd_ref, sm_ref,
    vTe, kn, dkT, dvT, gT, gc_buf, gi_buf, gi_pos, sm_buf, sm_seq, gb_buf, gqv_buf, gq_buf, gq_got, gq_fin,
    mine0, mine1, mine2, core0, core1, core2, yb0, yb1, yb2, zb0, zb1, zb2, xm0, xm1, xm2, xb0, xb1, xb2, f0, f1, f2, fb0, fb1, fb2,
    g_send, g_recv, i_send, i_recv, sm_send, sm_recv, ss_send, ss_recv, b_send, b_recv, bs_send, bs_recv,
    q_send, q_recv, qs_send, qs_recv, c_send, c_recv, y_send, y_recv, z_send, z_recv, xs_send, xs_recv, p_send, p_recv, own, local,
):
    heads = kn.shape[0]
    sources, rows, _ = x_ref.shape
    gw = heads * HD
    slot = sources * 2 * rows
    parts_q = gq_buf.shape[0]
    u = pl.program_id(0)
    i = lax.axis_index("dp")
    me = lax.axis_index("seq")
    c = lax.rem(me, 2)
    y = lax.rem(i, 2)
    k = i // 2
    depth = n // 2
    across = lax.rem(me + 2, sources)
    every = slice(None)
    inputs = (gwo_in, gwu_in, gwd_in)
    outputs = (gwo_ref, gwu_ref, gwd_ref)
    mine, core, ybuf, zbuf = (mine0, mine1, mine2), (core0, core1, core2), (yb0, yb1, yb2), (zb0, zb1, zb2)
    xmine, xbuf, final, fbuf = (xm0, xm1, xm2), (xb0, xb1, xb2), (f0, f1, f2), (fb0, fb1, fb2)

    def g_copy(d):
        peer = lax.rem(me + d, sources)
        return remote(gctx_in.at[peer], gc_buf.at[sources - 1 - d], g_send.at[d - 1], g_recv.at[d - 1], i, peer)

    def i_copy(d):
        return remote(gi_buf.at[d - 1], gi_pos.at[me], i_send.at[d - 1], i_recv.at[d - 1], i, lax.rem(me + d, sources))

    def sm_copy(d):
        to = lax.rem(i + d, n)
        return remote(sm_in.at[to], sm_buf.at[d - 1], sm_send.at[d - 1], sm_recv.at[d - 1], to, me)

    def ss_copy(d):
        return remote(sm_seq.at[me], sm_seq.at[me], ss_send.at[d - 1], ss_recv.at[d - 1], i, lax.rem(me + d, sources))

    def b_copy(d):
        return remote(gb_buf.at[i], gb_buf.at[i], b_send.at[d - 1], b_recv.at[d - 1], lax.rem(i + d, n), me)

    def bs_copy(d):
        return remote(gqv_buf, gqv_buf, bs_send.at[d - 1], bs_recv, i, lax.rem(me + d, sources))

    def q_copy(piece):
        to = me * parts_q + piece
        d = lax.rem(to - i + n, n)
        at = jnp.maximum(d, 1) - 1
        return d, remote(gq_buf.at[piece], gq_got.at[at], q_send.at[piece], q_recv.at[at], to, me)

    def qs_copy(d):
        return remote(gq_fin, gq_fin, qs_send.at[d - 1], qs_recv, i, lax.rem(me + d, sources))

    def own_copy(w):
        return pltpu.make_async_copy(half_of(inputs[w], (every, every), c), mine[w], own.at[w])

    def c_copy(w):
        return remote(half_of(inputs[w], (every, every), 1 - c), core[w], c_send.at[w], c_recv.at[w], i, other(me))

    def y_copy(w):
        return remote(mine[w].at[:, 1 - y], ybuf[w], y_send.at[w], y_recv.at[w], other(i), me)

    def z_copy(w, d):
        to = lax.rem(k + d, depth)
        return remote(mine[w].at[to, y], zbuf[w].at[d - 1], z_send.at[w, d - 1], z_recv.at[w, d - 1], to * 2 + y, me)

    def x_copy(w):
        return remote(xmine[w], xbuf[w], xs_send.at[w], xs_recv.at[w], i, across)

    def p_copy(w):
        return remote(final[w], fbuf[w], p_send.at[w], p_recv.at[w], i, other(me))

    g_own = pltpu.make_async_copy(gctx_in.at[me], gc_buf.at[sources - 1], local.at[0])
    sm_own = pltpu.make_async_copy(sm_in.at[i], sm_buf.at[n - 1], local.at[1])
    owner = i // parts_q == me
    count = gw // per
    bias_owner = lax.rem(i // count, GROUPS) == me

    def add(a, b):
        return (a.astype(F32) + b.astype(F32)).astype(BF16)

    def step_y(w):
        own_copy(w).wait()
        c_copy(w).wait_recv()
        mine[w][:, 1 - y] = add(mine[w][:, 1 - y], core[w][:, 1 - y])
        mine[w][:, y] = add(mine[w][:, y], core[w][:, y])
        y_copy(w).start()

    def step_z(w):
        y_copy(w).wait_recv()
        mine[w][:, y] = add(mine[w][:, y], ybuf[w][...])
        for d in range(1, depth):
            z_copy(w, d).start()

    def step_x(w):
        total = mine[w][k, y].astype(F32)
        for d in range(1, depth):
            z_copy(w, d).wait_recv()
            total += zbuf[w][d - 1].astype(F32)
        xmine[w][...] = total.astype(BF16)
        x_copy(w).start()

    def step_p(w):
        x_copy(w).wait_recv()
        final[w][...] = xmine[w][...].astype(F32) + xbuf[w][...].astype(F32)
        p_copy(w).start()

    def small_sum():
        sm_own.wait()
        total = sm_buf[n - 1]
        for d in range(1, n):
            sm_copy(d).wait_recv()
            total += sm_buf[d - 1]
        sm_seq[me] = total
        for d in range(1, sources):
            ss_copy(d).start()

    @pl.when(u == 0)
    def _():
        greet(n, sources, i, me)
        for d in (1, 2, 3):
            g_copy(d).start()
        g_own.start()
        for w in range(3):
            c_copy(w).start()
            own_copy(w).start()
        sm_own.start()
        for d in range(1, n):
            sm_copy(d).start()
        dkT[...] = jnp.zeros_like(dkT)
        dvT[...] = jnp.zeros_like(dvT)
        row = lax.broadcasted_iota(jnp.int32, (HD, slot), 0)
        ones_rows = jnp.where(row < 2, 1.0, 0.0).astype(BF16)
        for h in range(heads):
            cols = slice(h * HD, (h + 1) * HD)
            vTe[h, 0:HD, :] = vT_ref[cols, :]
            vTe[h, HD:, :] = ones_rows
            kn[h] = k_ref[:, cols]
        g_own.wait()

    for d in range(1, sources):
        @pl.when(u == d)
        def _(d=d):
            g_copy(d).wait_recv()

    plan = {
        (0, 2): [(step_y, 0)], (0, 3): [(step_y, 1)], (0, 4): [(step_y, 2)],
        (1, 4): [(step_z, 0)], (2, 3): [(step_z, 1)], (2, 5): [(step_x, 0)],
        (3, 2): [(step_z, 2)], (3, 4): [(step_x, 1)], (3, 5): [(step_p, 0)],
    }

    lane = lax.broadcasted_iota(jnp.int32, (rows, HD), 1)
    j = sources - 1 - u
    for half in range(2):
        at = pl.multiple_of((j * 2 + half) * rows, rows)
        lanes = slice(half * gw, (half + 1) * gw)
        g = gc_buf[j, :, lanes].astype(F32) * linv_ref[0, half]
        g_low = g.astype(BF16)
        gT_low = g_low.T
        prod = g * ctx_ref[0, :, lanes].astype(F32)
        dqs = []
        for h in range(heads):
            for (when_u, point), actions in plan.items():
                if point == half * heads + h:
                    @pl.when(u == when_u)
                    def _(actions=actions):
                        for fn, w in actions:
                            fn(w)
            if half * heads + h == 1:
                @pl.when(u == 1)
                def _():
                    small_sum()
            cols = slice(h * HD, (h + 1) * HD)
            delta = -jnp.sum(prod[:, cols], axis=1, keepdims=True)
            d_hi = delta.astype(BF16)
            d_lo = (delta - d_hi.astype(F32)).astype(BF16)
            tail = jnp.where(lane == 0, d_hi, jnp.where(lane == 1, d_lo, jnp.zeros((), BF16)))
            ge = jnp.concatenate([g_low[:, cols], tail], axis=1)
            e = e_ref[h, half * rows : (half + 1) * rows, :]
            ds = (e.astype(F32) * mm(ge, vTe[h])).astype(BF16)
            dvT[cols, :] += mm(gT_low[cols, :], e)
            dkT[cols, :] += mm(qT_ref[cols, half * rows : (half + 1) * rows], ds)
            dqs.append((mm(ds, kn[h]) * (HD ** (-0.5))).astype(BF16))
        gT[0:gw, pl.ds(at, rows)] = jnp.concatenate(dqs, axis=1).T

    @pl.when(u == sources - 1)
    def _():
        gT[gw : 2 * gw, :] = (dkT[...] * (HD ** (-0.5))).astype(BF16)
        gT[2 * gw :, :] = dvT[...].astype(BF16)
        gb_buf[i] = mm_nt(jnp.ones((8, slot), BF16), gT[...])
        ready = 0
        for q in (1, 0, 2, 3):
            packed = [
                mm(w_ref[...], gT[:, (q * 2 + half) * rows : (q * 2 + half + 1) * rows]).T.astype(BF16)
                for half in range(2)
            ]
            block = jnp.concatenate(packed, axis=1)
            if ready:
                i_copy(ready).start()
            if q < sources - 1:
                gi_buf[q] = block
            else:
                gi_pos[me] = block
            ready = q + 1
        for d in range(1, n):
            b_copy(d).start()
        sums = [None, None]
        for q in range(sources):
            for half in range(2):
                part = mm(gT[:, (q * 2 + half) * rows : (q * 2 + half + 1) * rows], x_ref[q, :, window(half)])
                sums[half] = part if sums[half] is None else sums[half] + part
        gq = (sums[0][:, :gw] + sums[1][:, 64:]).T
        size = gw // parts_q
        for piece in range(parts_q):
            gq_buf[piece] = gq[piece * size : (piece + 1) * size].astype(BF16)
        step_x(2)
        for piece in range(parts_q):
            d, copy = q_copy(piece)

            @pl.when(d != 0)
            def _():
                copy.start()

        step_p(1)

        for d in range(1, n):
            b_copy(d).wait_recv()

        @pl.when(bias_owner)
        def _():
            total = gb_buf[0, 0:1, :]
            for d in range(1, n):
                total += gb_buf[d, 0:1, :]
            side = jnp.where(i < n // 2, total[:, :gw], total[:, 2 * gw :])
            piece = lax.rem(i, count)
            value = side[:, 0:per]
            for v in range(1, count):
                value = jnp.where(piece == v, side[:, v * per : (v + 1) * per], value)
            gqv_buf[0:1, 0:per] = value
            for d in range(1, sources):
                bs_copy(d).start()

        step_p(2)

        @pl.when(owner)
        def _():
            total = gq_buf[jnp.clip(i - me * parts_q, 0, parts_q - 1)].astype(F32)
            for d in range(1, n):
                remote(gq_buf.at[0], gq_got.at[d - 1], q_send.at[0], q_recv.at[d - 1], other(i), me).wait_recv()
                total += gq_got[d - 1].astype(F32)
            gq_fin[...] = total.astype(BF16)
            for d in range(1, sources):
                qs_copy(d).start()

        for d in range(1, sources):
            ss_copy(d).wait_recv()
        total = sm_seq[0]
        for v in range(1, sources):
            total += sm_seq[v]
        sm_ref[...] = total
        for w in range(3):
            p_copy(w).wait_recv()
            ref = outputs[w]
            for v in range(2):
                value = jnp.where(c == v, final[w][...], fbuf[w][...])
                if len(ref.shape) == 3:
                    ref[v] = value
                else:
                    half = ref.shape[1] // 2
                    ref[:, v * half : (v + 1) * half] = value

        for d in range(1, sources):
            i_copy(d).wait_recv()
        for half in range(2):
            r = slice(half * rows, (half + 1) * rows)
            lanes = slice(half * gw, (half + 1) * gw)
            for pair in range(GROUPS // 2):
                both = jnp.concatenate([gi_pos[2 * pair, :, lanes], gi_pos[2 * pair + 1, :, lanes]], axis=1)
                wide = slice(pair * 2 * gw, (pair + 1) * 2 * gw)
                gt_ref[r, wide] = (both.astype(F32) + gres_ref[r, wide]).astype(BF16)

        @pl.when(jnp.logical_not(bias_owner))
        def _():
            bs_copy(1).wait_recv()

        gqv_ref[...] = gqv_buf[0:1, 0:per]

        @pl.when(jnp.logical_not(owner))
        def _():
            qs_copy(1).wait_recv()

        gqkv_ref[...] = gq_fin[...].astype(F32)

        for d in range(1, sources):
            g_copy(d).wait_send()
            i_copy(d).wait_send()
            ss_copy(d).wait_send()

        @pl.when(bias_owner)
        def _():
            for d in range(1, sources):
                bs_copy(d).wait_send()

        @pl.when(owner)
        def _():
            for d in range(1, sources):
                qs_copy(d).wait_send()

        for piece in range(parts_q):
            d, copy = q_copy(piece)

            @pl.when(d != 0)
            def _():
                copy.wait_send()

        for d in range(1, n):
            sm_copy(d).wait_send()
            b_copy(d).wait_send()
        for w in range(3):
            c_copy(w).wait_send()
            y_copy(w).wait_send()
            for d in range(1, depth):
                z_copy(w, d).wait_send()
            x_copy(w).wait_send()
            p_copy(w).wait_send()


def revisit(n, per, e, ctx, linv, qT, vT, k, x, w, gres, gctx, gwo, gwu, gwd, small):
    sources, rows, _ = x.shape
    gw = w.shape[0]
    heads = gw // HD
    slot = sources * 2 * rows
    parts_q = n // GROUPS
    depth = n // 2
    last = sources - 1
    whole = lambda *shape: pl.BlockSpec(shape, lambda s: (0,) * len(shape), pipeline_mode=pl.Buffered(1))
    out_whole = lambda *shape: pl.BlockSpec(shape, lambda s: (0,) * len(shape))
    anywhere = pl.BlockSpec(memory_space=pl.ANY)
    dma = lambda *shape: pltpu.SemaphoreType.DMA(shape)

    def half_shape(a):
        return a.shape[3:] if len(a.shape) == 5 else (a.shape[2], a.shape[3] // 2)

    halves = [half_shape(a) for a in (gwo, gwu, gwd)]
    outs = [
        jax.ShapeDtypeStruct((2 * rows, GROUPS * gw), BF16),
        jax.ShapeDtypeStruct((gw // parts_q, 3 * gw), F32),
        jax.ShapeDtypeStruct((1, per), F32),
        jax.ShapeDtypeStruct(gwo.shape[2:], F32),
        jax.ShapeDtypeStruct(gwu.shape[2:], F32),
        jax.ShapeDtypeStruct(gwd.shape[2:], F32),
        jax.ShapeDtypeStruct(small.shape[1:], F32),
    ]
    vmem = pltpu.VMEM
    return pl.pallas_call(
        functools.partial(revisit_kernel, n, per),
        grid=(sources,),
        in_specs=[
            pl.BlockSpec((heads, 2 * rows, slot), lambda s: (0, last - s, 0)),
            pl.BlockSpec((1, rows, 2 * gw), lambda s: (last - s, 0, 0)),
            pl.BlockSpec((1, 2, rows, gw), lambda s: (last - s, 0, 0, 0)),
            pl.BlockSpec((gw, 2 * rows), lambda s: (0, last - s)),
            whole(*vT.shape), whole(*k.shape), whole(*x.shape), whole(*w.shape), whole(*gres.shape),
            anywhere, anywhere, anywhere, anywhere, anywhere,
        ],
        out_specs=[out_whole(*o.shape) for o in outs],
        out_shape=outs,
        scratch_shapes=[
            vmem((heads, 2 * HD, slot), BF16),
            vmem((heads, slot, HD), BF16),
            vmem((gw, slot), F32),
            vmem((gw, slot), F32),
            vmem((3 * gw, slot), BF16),
            vmem(x.shape, BF16), vmem((sources - 1,) + x.shape[1:], BF16), vmem(x.shape, BF16),
            vmem(small.shape, F32), vmem((sources,) + small.shape[1:], F32),
            vmem((n, 8, 3 * gw), F32), vmem((8, 256), F32),
            vmem((parts_q, gw // parts_q, 3 * gw), BF16),
            vmem((n - 1, gw // parts_q, 3 * gw), BF16),
            vmem((gw // parts_q, 3 * gw), BF16),
        ]
        + [vmem((depth, 2) + s, BF16) for s in halves]
        + [vmem((depth, 2) + s, BF16) for s in halves]
        + [vmem((depth,) + s, BF16) for s in halves]
        + [vmem((depth - 1,) + s, BF16) for s in halves]
        + [vmem(s, BF16) for s in halves]
        + [vmem(s, BF16) for s in halves]
        + [vmem(s, F32) for s in halves]
        + [vmem(s, F32) for s in halves]
        + [
            dma(3), dma(3), dma(3), dma(3), dma(n - 1), dma(n - 1), dma(3), dma(3), dma(n - 1), dma(n - 1),
            dma(3), pltpu.SemaphoreType.DMA, dma(parts_q), dma(n - 1), dma(3), pltpu.SemaphoreType.DMA,
            dma(3), dma(3), dma(3), dma(3), dma(3, depth - 1), dma(3, depth - 1), dma(3), dma(3), dma(3), dma(3), dma(3), dma(2),
        ],
        compiler_params=pltpu.CompilerParams(vmem_limit_bytes=62 << 20, collective_id=2, has_side_effects=True),
        name="revisit",
    )(e, ctx, linv, qT, vT, k, x, w, gres, gctx, gwo, gwu, gwd, small)


def split_rows(values):
    mean = jnp.mean(values, axis=-1, keepdims=True)
    centred = values - mean
    var = jnp.mean(centred * centred, axis=-1, keepdims=True)
    return centred, lax.rsqrt(var + epsilon)


def norm_back(grad, unit, inverse, gain):
    g = grad * gain
    m1 = jnp.mean(g, axis=-1, keepdims=True)
    m2 = jnp.mean(g * unit, axis=-1, keepdims=True)
    return inverse * (g - m1 - unit * m2)


def join_windows(parts):
    tiles = []
    for even, odd in zip(parts[0::2], parts[1::2]):
        tiles += [even[:, :128], even[:, 128:] + odd[:, :128], odd[:, 128:]]
    return jnp.concatenate(tiles, axis=1)


def group_window(g):
    at = (g // 2) * 384 + (g % 2) * 128
    return slice(at, at + 256)


def middle_kernel(
    n, pos_ref, ctx_ref, tok_ref, gout_ref, wo_ref, wu_ref, wd_ref, vec_ref,
    out_ref, gctx_ref, gres_ref, gwo_ref, gwu_ref, gwd_ref, small_ref, upad, dpad, awo, awu, awd, sums, usums,
):
    rows = ctx_ref.shape[1]
    gw = ctx_ref.shape[2] // 2
    width = tok_ref.shape[1]
    hidden = wu_ref.shape[1]
    share = width // n
    vec = join_lanes([vec_ref[d, :, 0:share] for d in range(n)])
    obias, gain1, shift1, dbias, gain2, shift2 = (vec[v : v + 1] for v in range(1, 7))
    count = n // GROUPS
    for g in range(GROUPS):
        upad[g] = pad_rows(wu_ref[g * gw : (g + 1) * gw, :], g % 2)
        dpad[g] = pad_lanes(wd_ref[g * hidden : (g + 1) * hidden, :], g % 2)
    packed = [[] for _ in range(GROUPS)]
    for half in range(2):
        first = half == 0

        def keep(ref, at, value):
            if first:
                ref[at] = value
            else:
                ref[at] += value

        r = slice(half * rows, (half + 1) * rows)
        x = tok_ref[r, :].astype(F32) + obias
        for g in range(GROUPS):
            x += mm(ctx_ref[g, :, window(half)], pad_rows(wo_ref[g * gw : (g + 1) * gw, :], half))
        c1, i1 = split_rows(x)
        n1 = c1 * i1
        mixed = n1 * gain1 + shift1
        low = mixed.astype(BF16)
        lowered = []
        slopes = []
        actives = []
        for g in range(GROUPS):
            ub = join_lanes([vec_ref[g * count + d, 7:8, 0 : hidden // count] for d in range(count)])
            u = mm(low[:, group_window(g)], upad[g]) + ub
            phi = 0.5 + 0.5 * lax.erf(u * (0.5 ** 0.5))
            slope = phi + u * (jnp.exp(u * u * -0.5) * 0.3989422804014327)
            act = (u * phi).astype(BF16)
            actives.append(act)
            slopes.append(slope)
            lowered.append(mm(act, dpad[g]))
        x = mixed + join_windows(lowered) + dbias
        c2, i2 = split_rows(x)
        n2 = c2 * i2
        row = lax.broadcasted_iota(jnp.int32, (rows, 1), 0) + (pos_ref[1] + half * rows)
        valid = jnp.where(row < pos_ref[0], 1.0, 0.0)
        out_ref[r, :] = (valid * (n2 * gain2 + shift2)).astype(BF16)
        gy = gout_ref[r, :].astype(F32) * valid
        d2 = norm_back(gy, n2, i2, gain2)
        keep(sums, slice(4, 5), jnp.sum(gy * n2, axis=0, keepdims=True))
        keep(sums, slice(5, 6), jnp.sum(gy, axis=0, keepdims=True))
        keep(sums, slice(3, 4), jnp.sum(d2, axis=0, keepdims=True))
        d2_low = d2.astype(BF16)
        backs = []
        for g in range(GROUPS):
            win = d2_low[:, group_window(g)]
            odd = 64 * (g % 2)
            part = mm_tn(actives[g], win)
            if first:
                awd[g] = part
            else:
                gwd_ref[g * hidden : (g + 1) * hidden, :] = (awd[g] + part)[:, odd : odd + gw].astype(BF16)
            gu = mm_nt(win, dpad[g]) * slopes[g]
            keep(usums, slice(g, g + 1), jnp.sum(gu, axis=0, keepdims=True))
            gu_low = gu.astype(BF16)
            part = mm_tn(low[:, group_window(g)], gu_low)[odd : odd + gw]
            if first:
                awu[g] = part
            else:
                gwu_ref[g * gw : (g + 1) * gw, :] = (awu[g] + part).astype(BF16)
            backs.append(mm_nt(gu_low, upad[g]))
        gm = join_windows(backs) + d2
        d1 = norm_back(gm, n1, i1, gain1)
        keep(sums, slice(1, 2), jnp.sum(gm * n1, axis=0, keepdims=True))
        keep(sums, slice(2, 3), jnp.sum(gm, axis=0, keepdims=True))
        keep(sums, slice(0, 1), jnp.sum(d1, axis=0, keepdims=True))
        gres_ref[r, :] = d1
        d1_low = d1.astype(BF16)
        for g in range(GROUPS):
            part = mm_tn(ctx_ref[g, :, window(half)], d1_low)[64 * half : 64 * half + gw]
            if first:
                awo[g] = part
            else:
                gwo_ref[g * gw : (g + 1) * gw, :] = (awo[g] + part).astype(BF16)
        back = mm_nt(d1_low, wo_ref[...]).astype(BF16)
        for g in range(GROUPS):
            packed[g].append(back[:, g * gw : (g + 1) * gw])
    for g in range(GROUPS):
        gctx_ref[g] = jnp.concatenate(packed[g], axis=1)
    sums[6:8, :] = jnp.zeros((2, width), F32)
    up_share = hidden // count
    for d in range(n):
        small_ref[d] = jnp.zeros(small_ref.shape[1:], F32)
        small_ref[d, 0:8, 0:share] = sums[0:8, d * share : (d + 1) * share]
        at = (d % count) * up_share
        for v in range(0, up_share, 128):
            size = min(128, up_share - v)
            small_ref[d, 8 + v // 128 : 9 + v // 128, 0:size] = usums[d // count : d // count + 1, at + v : at + v + size]


def middle(n, pos, ctx, tok, gout, wo, wu, wd, vec):
    hidden = wu.shape[1]
    width = tok.shape[1]
    gw = width // GROUPS
    vmem = pl.BlockSpec(memory_space=pltpu.VMEM)
    return pl.pallas_call(
        functools.partial(middle_kernel, n),
        in_specs=[pl.BlockSpec(memory_space=pltpu.SMEM)] + [vmem] * 7,
        out_specs=[vmem] * 7,
        out_shape=[
            jax.ShapeDtypeStruct(tok.shape, BF16),
            jax.ShapeDtypeStruct(ctx.shape, BF16),
            jax.ShapeDtypeStruct(tok.shape, F32),
            jax.ShapeDtypeStruct(wo.shape, BF16),
            jax.ShapeDtypeStruct(wu.shape, BF16),
            jax.ShapeDtypeStruct(wd.shape, BF16),
            jax.ShapeDtypeStruct((n, 16, 128), F32),
        ],
        scratch_shapes=[
            pltpu.VMEM((GROUPS, 256, hidden), BF16),
            pltpu.VMEM((GROUPS, hidden, 256), BF16),
            pltpu.VMEM((GROUPS, gw, width), F32),
            pltpu.VMEM((GROUPS, gw, hidden), F32),
            pltpu.VMEM((GROUPS, hidden, 256), F32),
            pltpu.VMEM((8, width), F32),
            pltpu.VMEM((8, hidden), F32),
        ],
        compiler_params=pltpu.CompilerParams(vmem_limit_bytes=62 << 20),
        name="middle",
    )(pos, ctx, tok, gout, wo, wu, wd, vec)


def on_device(
    tokens, lengths, qkv_weight, qv_bias, out_weight, out_bias, norm_gain, norm_shift,
    up_weight, up_bias, down_weight, down_bias, final_gain, final_shift, grad_output,
):
    n = lax.axis_size("dp")
    _, piece_rows, width = tokens.shape
    gw = width // GROUPS
    half = piece_rows // 2
    share, per, up_share = out_bias.shape[0], qv_bias.shape[0], up_bias.shape[0]
    me = lax.axis_index("seq")
    lanes = -(-max(up_share, per) // 128) * 128
    vec = jnp.stack([
        jnp.pad(a.astype(F32), (0, lanes - a.shape[0]))
        for a in (qv_bias, out_bias, norm_gain, norm_shift, down_bias, final_gain, final_shift, up_bias)
    ])
    x = tokens.reshape(2, half, GROUPS, gw).transpose(2, 1, 0, 3).reshape(GROUPS, half, 2 * gw)
    wd_halves = down_weight.reshape(2, down_weight.shape[0] // 2, gw)
    ctx, linv, e, k, qT, vT, w, vecs, x_all, ctx_pos, wo, wu, wd = attend(
        n, per, lengths, x, qkv_weight, vec, out_weight, up_weight, wd_halves
    )
    pos = jnp.stack([lengths[0], (me * piece_rows).astype(jnp.int32)])
    output, gctx, gres, gwo, gwu, gwd, small = middle(
        n, pos, ctx_pos, tokens[0], grad_output[0],
        wo.reshape(width, width), wu.reshape(width, -1), wd.reshape(-1, gw), vecs,
    )
    grad_tokens, gqkv, gqv, gwo, gwu, gwd, small = revisit(
        n, per, e, ctx, linv, qT, vT, k, x_all, w, gres, gctx,
        gwo.reshape(wo.shape), gwu.reshape(wu.shape), gwd.reshape(wd.shape), small,
    )
    return (
        output[None], grad_tokens[None], gqkv, gqv[0], gwo, small[0, :share],
        small[1, :share], small[2, :share], gwu, small[8:].reshape(-1)[:up_share], gwd.reshape(down_weight.shape),
        small[3, :share], small[4, :share], small[5, :share],
    )


def solution(mesh):
    rows = P("dp", "seq", None)
    mat = P("dp", None)
    vec = P("dp")
    in_specs = (rows, vec, mat, vec, mat, vec, vec, vec, mat, vec, mat, vec, vec, vec, rows)
    out_specs = (rows, rows, mat, vec, mat, vec, vec, vec, mat, vec, mat, vec, vec, vec)
    return jax.shard_map(on_device, mesh=mesh, in_specs=in_specs, out_specs=out_specs, check_vma=False)
```

time: 586 us -> 173 us (0.30)
  waiting for transfers between devices: 273 us -> 0 us
  blocking collectives: 157 us -> 0 us
  Pallas kernels: 76.8 us -> 148 us
  between operations: 18.8 us -> 1.37 us
  local copies, waits for them, and re-layouts: 32.5 us -> 19.4 us
  starting transfers between devices: 11.6 us -> 0 us
  other arithmetic: 7.06 us -> 1.19 us
    reduce_scatter x4 -> x0, waiting for transfers between devices: 271 us -> none  [total(): lax.psum_scatter(a, 'dp', scatter_dimension=0, tiled=True)]
    unnamed x2 -> x0, blocking collectives: 74 us -> none
    pallas_call x3, Pallas kernels: 76.8 us -> 148 us  [the longest x1 68.9 us: revisit(): pl.pallas_call(functools.partial(revisit_kernel, n, per), grid=(sources,)...]
    all_gather x2 -> x0, blocking collectives: 60.9 us -> none  [on_device(): gather = lambda a: lax.all_gather(a, 'dp', axis=0, tiled=True)]
    all_to_all x1 -> x0, blocking collectives: 15.9 us -> none  [swap(): return lax.all_to_all(t, 'seq', split_axis=0, concat_axis=0, tiled=True)]
    all_to_all x3 -> x0, starting transfers between devices: 11.2 us -> none  [swap(): return lax.all_to_all(t, 'seq', split_axis=0, concat_axis=0, tiled=True)]
    unnamed x60 -> x16, local copies, waits for them, and re-layouts: 17.8 us -> 9.8 us
    psum x1 -> x0, blocking collectives: 6.56 us -> none  [total(): lax.psum(lax.psum_scatter(a, 'dp', scatter_dimension=0, tiled=True), 'seq')]
  transfers between devices with their start and end apart: 11 -> 0, of which waited for: 4 -> 0; matrix products, arithmetic and copies ran while one was open for 4% -> 0% of each run, Pallas kernels for 5% -> 0%
where the time goes in v2:
time: 173 us; the launch traced here: 170 us
  Pallas kernels  148 us (86%)
  local copies, waits for them, and re-layouts  19.4 us (11%)
    pallas_call x1, Pallas kernels, revisit(): pl.pallas_call(functools.partial(revisit_kernel, n, per), grid=(sources,)...  68.9 us
    pallas_call x1, Pallas kernels, attend(): pl.pallas_call(functools.partial(attend_kernel, n, per), grid=(sources,),...  61.2 us
    pallas_call x1, Pallas kernels, middle(): pl.pallas_call(functools.partial(middle_kernel, n), in_specs=[pl.BlockSpe...  17.5 us
    unnamed x16, local copies, waits for them, and re-layouts  9.8 us
    pad x7, local copies, waits for them, and re-layouts, on_device(): jnp.pad(a.astype(F32), (0, lanes - a.shape[0]))  4.62 us

profile of v2, /device:TPU:0, one launch (start us, length us, event | category | flops | bytes accessed | tf_op | source)
XLA Modules:
  0.0 169.6 jit_solution(10063824548007528656)
XLA Ops:
  1.3 0.6 pad_add_fusion.pos_ref
  1.9 0.7 pad.30
  2.5 0.7 pad.31
  3.2 0.7 pad.32
  3.9 0.7 pad.33
  4.6 0.7 pad.34
  5.2 0.7 pad.35
  5.9 0.7 pad.36
  6.6 0.7 stack.52
  7.3 0.6 stack.54.vec_in
  7.9 1.7 %copy.34 = bf16[384,192]{1,0:T(8,128)(2,1)} copy(bf16[384,192]{0,1:T(8,128)(2,1)} %param.25) | data formatting | bytes 294912 | tf_op args[10]
  9.6 1.4 copy.32
  11.0 0.2 reshape.60
  11.2 0.1 copy.33
  11.3 1.2 copy.35.x_in
  12.5 61.2 %attend.1 = (bf16[4,256,384]{2,1,0:T(8,128)(2,1)}, f32[4,2,256,192]{3,2,1,0:T(8,128)}, bf16[3,2048,2048]{2,1,0:T(8,128)(2,1)}, bf16[2048,192]{1,0:T(8,128)(2,1)}...) custom-call(s32[1]{0:T(128)S(6)} %copy.42.len_ref, ...), custom_call_target="tpu_custom_call" | custom-call | tf_op jit(solution)/shard_map/attend/pallas_call | solution.py:308
  73.7 17.5 %middle.1 = (bf16[512,768]{1,0:T(8,128)(2,1)}, bf16[4,256,384]{2,1,0:T(8,128)(2,1)}, f32[512,768]{1,0:T(8,128)}, bf16[768,768]{1,0:T(8,128)(2,1)}, bf16[768,768]...) custom-call(s32[2]{0:T(128)} %pad_add_fusion.pos_ref, ...), custom_call_target="tpu_custom_call" | custom-call | tf_op jit(solution)/shard_map/middle/pallas_call | solution.py:894
  91.2 68.9 %revisit.1 = (bf16[512,768]{1,0:T(8,128)(2,1)}, f32[96,576]{1,0:T(8,128)}, f32[1,192]{1,0:T(1,128)}, f32[96,768]{1,0:T(8,128)}, f32[96,768]{1,0:T(8,128)}, /*index=5*/f32[2,192,192]{2,1,0:T(8,128)}, f32[16,128]{1,0:T(8,128)}) custom-call(bf16[3,2048,2048]{2,1,0:T(8,128)(2,1)} %get-tuple-element.47.e_ref, bf16[4,256,384]{2,1,0:T(8,128)(2,1)} %get-tuple-element.48.ctx_ref, ...), custom_call_target="tpu_custom_call" | custom-call | tf_op jit(solution)/shard_map/revisit/pallas_call | solution.py:715
  160.1 0.0 copy-start.2
  160.1 0.0 copy-start.3
  160.1 0.0 copy-start.1
  160.2 1.3 slice_bitcast_fusion
  161.5 1.4 slice_bitcast_fusion.1
  162.9 0.0 copy-start
  162.9 1.9 %copy.36 = f32[384,192]{0,1:T(8,128)} copy(f32[384,192]{1,0:T(8,128)} %bitcast.44) | data formatting | bytes 589824
  164.8 2.1 %copy.43 = bf16[1,512,768]{2,1,0:T(8,128)(2,1)} copy(bf16[1,512,768]{2,1,0:T(8,128)(2,1)} %bitcast.42) | data formatting | bytes 1572864
  166.9 0.0 copy-done.2
  166.9 0.7 copy.44
  167.6 0.0 copy-done.3
  167.6 0.6 copy.45
  168.1 0.0 copy-done.1
  168.1 0.7 copy.46
  168.9 0.0 copy-done
  168.9 0.7 copy.47
  (8 shorter events, 0.1 us)
Async XLA Ops:
  160.1 6.8 %copy-start.2 = (f32[96,576]{1,0:T(8,128)S(1)}, f32[96,576]{1,0:T(8,128)}, u32[]{:S(2)}) copy-start(f32[96,576]{1,0:T(8,128)} %get-tuple-element.118) | copy-start | bytes 663556
  160.1 7.4 %copy-start.3 = (f32[1,192]{1,0:T(1,128)S(1)}, f32[1,192]{1,0:T(1,128)}, u32[]{:S(2)}) copy-start(f32[1,192]{1,0:T(1,128)} %get-tuple-element.63) | copy-start | bytes 2308
  160.1 8.0 %copy-start.1 = (f32[96,768]{1,0:T(8,128)S(1)}, f32[96,768]{1,0:T(8,128)}, u32[]{:S(2)}) copy-start(f32[96,768]{1,0:T(8,128)} %get-tuple-element.120) | copy-start | bytes 884740
  162.9 6.0 %copy-start = (f32[96,768]{1,0:T(8,128)S(1)}, f32[96,768]{1,0:T(8,128)}, u32[]{:S(2)}) copy-start(f32[96,768]{1,0:T(8,128)} %get-tuple-element.124) | copy-start | bytes 884740

commit v3 on v2

v3 whole, which is shorter than its diff:
```python
import functools

import jax
import jax.numpy as jnp
from jax import lax
from jax.experimental import pallas as pl
from jax.experimental.pallas import tpu as pltpu
from jax.sharding import PartitionSpec as P

H = 12
GROUPS = 4
HD = 64
epsilon = 1e-05
LOG2E = 1.4426950408889634
MASKED = -1e30
F32 = jnp.float32
BF16 = jnp.bfloat16


def mm(a, b):
    return jnp.dot(a, b, preferred_element_type=F32)


def mm_nt(a, b):
    return lax.dot_general(a, b, (((1,), (1,)), ((), ())), preferred_element_type=F32)


def mm_tn(a, b):
    return lax.dot_general(a, b, (((0,), (0,)), ((), ())), preferred_element_type=F32)


def pad_rows(w, half):
    zeros = jnp.zeros((64, w.shape[1]), w.dtype)
    return jnp.concatenate([w, zeros] if half == 0 else [zeros, w], axis=0)


def pad_lanes(w, half):
    zeros = jnp.zeros((w.shape[0], 64), w.dtype)
    return jnp.concatenate([w, zeros] if half == 0 else [zeros, w], axis=1)


def window(half):
    return slice(half * 128, half * 128 + 256)


MESH = pl.DeviceIdType.MESH


def remote(src, dst, send_sem, recv_sem, dp, seq):
    return pltpu.make_async_remote_copy(
        src_ref=src, dst_ref=dst, send_sem=send_sem, recv_sem=recv_sem,
        device_id={"dp": dp, "seq": seq}, device_id_type=MESH,
    )


def greet(n, group, i, s):
    barrier = pltpu.get_barrier_semaphore()
    for d in range(1, n):
        pl.semaphore_signal(barrier, inc=1, device_id={"dp": lax.rem(i + d, n), "seq": s}, device_id_type=MESH)
    for d in range(1, group):
        pl.semaphore_signal(barrier, inc=1, device_id={"dp": i, "seq": lax.rem(s + d, group)}, device_id_type=MESH)
    pl.semaphore_wait(barrier, n + group - 2)


def other(index):
    return index + 1 - 2 * lax.rem(index, 2)


def half_of(ref, lead, c):
    if len(ref.shape) == len(lead) + 3:
        return ref.at[lead + (c,)]
    lanes = ref.shape[-1] // 2
    at = pl.multiple_of(c * lanes, 128) if lanes % 128 == 0 else c * lanes
    return ref.at[lead + (slice(None), pl.ds(at, lanes))]


def stack_rows(pieces):
    if len(pieces) == 1:
        return pieces[0]
    if pieces[0].shape[0] % 16 == 0:
        return jnp.concatenate(pieces, axis=0)
    return jnp.concatenate([p.astype(F32) for p in pieces], axis=0).astype(pieces[0].dtype)


def join_lanes(pieces):
    return pieces[0] if len(pieces) == 1 else jnp.concatenate(pieces, axis=1)


def attend_kernel(
    n, len_ref, tok_ref, wq_in, wo_in, wu_in, wd_in, v0, v1, v2, v3, v4, v5, v6, v7,
    ctx_ref, linv_ref, e_ref, k_out, qT_out, vT_out, w_out, vec_out, x_out, ctx_pos, wo_out, wu_out, wd_out,
    qe, ke, ve, xp, x_buf, ctx_half, ctx_buf, q_part, wq_buf, vec_in, vec_buf,
    x_send, x_recv, c_send, c_recv, q_send, q_recv, r_send, r_recv, v_send, v_recv, z_send, z_recv, y_send, y_recv, p_send, p_recv, own, local,
):
    heads = qe.shape[0]
    sources, rows, _ = x_buf.shape
    gw = heads * HD
    slot = sources * 2 * rows
    per = v0.shape[-1]
    parts_q = wq_buf.shape[1]
    t = pl.program_id(0) // 2
    half_now = lax.rem(pl.program_id(0), 2)
    i = lax.axis_index("dp")
    me = lax.axis_index("seq")
    c = lax.rem(me, 2)
    y = lax.rem(i, 2)
    k = i // 2
    depth = n // 2
    weights = ((wo_in, wo_out), (wu_in, wu_out), (wd_in, wd_out))

    def x_copy(d):
        peer = lax.rem(me + d, sources)
        return remote(xp.at[peer], x_buf.at[sources - 1 - d], x_send.at[d - 1], x_recv.at[d - 1], i, peer)

    def ctx_copy(d):
        peer = lax.rem(me + d, sources)
        return remote(ctx_buf.at[d - 1], ctx_pos.at[me], c_send.at[d - 1], c_recv.at[d - 1], i, peer)

    def q_copy(d):
        return remote(wq_in.at[me], q_part.at[i], q_send.at[d - 1], q_recv.at[d - 1], lax.rem(i + d, n), me)

    def r_copy(d):
        peer = lax.rem(me + d, sources)
        return remote(
            q_part.at[pl.ds(peer * parts_q, parts_q)], wq_buf.at[me], r_send.at[d - 1], r_recv.at[d - 1], i, peer
        )

    def v_copy(d):
        return remote(vec_in, vec_buf.at[i], v_send.at[d - 1], v_recv.at[d - 1], lax.rem(i + d, n), me)

    def z_copy(w, d):
        src, dst = weights[w]
        to = lax.rem(k + d, depth)
        return remote(
            half_of(src, (), c), half_of(dst, (k, y), c), z_send.at[w, d - 1], z_recv.at[w, d - 1], to * 2 + y, me
        )

    def own_copy(w):
        src, dst = weights[w]
        return pltpu.make_async_copy(half_of(src, (), c), half_of(dst, (k, y), c), own.at[w])

    def y_copy(w):
        part = half_of(weights[w][1], (slice(None), y), c)
        return remote(part, part, y_send.at[w], y_recv.at[w], other(i), me)

    def p_copy(w):
        part = half_of(weights[w][1], (slice(None), slice(None)), c)
        return remote(part, part, p_send.at[w], p_recv.at[w], i, other(me))

    x_own = pltpu.make_async_copy(xp.at[me], x_buf.at[sources - 1], local.at[0])
    x_keep = pltpu.make_async_copy(x_buf, x_out, local.at[1])
    v_own = pltpu.make_async_copy(vec_in, vec_buf.at[i], local.at[2])
    ctx_own = pltpu.make_async_copy(ctx_buf.at[sources - 1], ctx_pos.at[me], local.at[3])
    q_own = pltpu.make_async_copy(wq_in.at[me], q_part.at[i], local.at[4])
    r_own = pltpu.make_async_copy(q_part.at[pl.ds(me * parts_q, parts_q)], wq_buf.at[me], local.at[5])

    def step_y(w):
        own_copy(w).wait()
        for d in range(1, depth):
            z_copy(w, d).wait_recv()
        y_copy(w).start()

    def step_p(w):
        y_copy(w).wait_recv()
        p_copy(w).start()

    @pl.when(pl.program_id(0) == 0)
    def _():
        for g in range(GROUPS):
            cols = slice(g * gw, (g + 1) * gw)
            xp[g] = jnp.concatenate([tok_ref[0:rows, cols], tok_ref[rows:, cols]], axis=1)
        vec_in[...] = jnp.zeros_like(vec_in)
        for v, ref in enumerate((v0, v1, v2, v3, v4, v5, v6, v7)):
            vec_in[v : v + 1, 0 : ref.shape[-1]] = ref[...].astype(F32).reshape(1, ref.shape[-1])
        greet(n, sources, i, me)
        for d in range(1, n):
            q_copy(d).start()
        q_own.start()
        x_copy(2).start()

        @pl.when(c == 0)
        def _():
            x_copy(1).start()

        @pl.when(c == 1)
        def _():
            x_copy(3).start()

        x_own.start()
        v_own.start()
        for d in range(1, n):
            v_copy(d).start()
        for w in range(3):
            for d in range(1, depth):
                z_copy(w, d).start()
            own_copy(w).start()

        scale = HD ** (-0.5) * LOG2E
        lane = lax.broadcasted_iota(jnp.int32, (slot, 128), 1)
        ones_lane = jnp.where(lane == 0, 1.0, 0.0).astype(BF16)
        key_row = lax.broadcasted_iota(jnp.int32, (128, 2 * rows), 0)
        for h in range(heads):
            qe[h, :, 128:256] = ones_lane
        for j in range(sources):
            first = lax.rem(me + 1 + j, sources) * (2 * rows)
            key_pos = lax.broadcasted_iota(jnp.int32, (128, 2 * rows), 1) + first
            bias = jnp.where((key_row == 0) & (key_pos >= len_ref[0]), MASKED, 0.0).astype(BF16)
            for h in range(heads):
                ke[h, 128:256, j * 2 * rows : (j + 1) * 2 * rows] = bias

        q_own.wait()
        for d in range(1, n):
            q_copy(d).wait_recv()
        for d in range(1, sources):
            r_copy(d).start()

        @pl.when(c == 0)
        def _():
            x_copy(3).start()

        @pl.when(c == 1)
        def _():
            x_copy(1).start()

        r_own.start()

        v_own.wait()
        for d in range(1, n):
            v_copy(d).wait_recv()
        vec_out[...] = vec_buf[...]
        count = gw // per
        q_bias = join_lanes([vec_buf[me * count + u, 0:1, 0:per] for u in range(count)])
        v_bias = join_lanes([vec_buf[(GROUPS + me) * count + u, 0:1, 0:per] for u in range(count)])
        b = jnp.concatenate([q_bias, jnp.zeros((1, gw), F32), v_bias], axis=1)
        r_own.wait()
        for d in range(1, sources):
            r_copy(d).wait_recv()
        weight = stack_rows([wq_buf[v, u] for u in range(parts_q) for v in range(sources)])
        w_out[...] = weight
        x_own.wait()
        for j in (3, 1, 2, 0):
            if j < sources - 1:
                x_copy(sources - 1 - j).wait_recv()
            for half in range(2):
                at = (j * 2 + half) * rows
                w = pad_rows(weight, half)
                qkv = (mm(x_buf[j, :, window(half)], w) + b).astype(BF16)
                q = qkv[:, :gw]
                kk = qkv[:, gw : 2 * gw]
                v = qkv[:, 2 * gw :]
                k_out[at : at + rows, :] = kk
                qT_out[:, at : at + rows] = q.T
                vT_out[:, at : at + rows] = v.T
                kT = kk.T
                scaled = q.astype(F32) * scale
                hi = scaled.astype(BF16)
                lo = (scaled - hi.astype(F32)).astype(BF16)
                ones = jnp.ones((rows, HD), BF16)
                for h in range(heads):
                    cols = slice(h * HD, (h + 1) * HD)
                    qe[h, at : at + rows, 0:128] = jnp.concatenate([hi[:, cols], lo[:, cols]], axis=1)
                    ke[h, 0:HD, at : at + rows] = kT[cols, :]
                    ke[h, HD : 2 * HD, at : at + rows] = kT[cols, :]
                    ve[h, at : at + rows, :] = jnp.concatenate([v[:, cols], ones], axis=1)
        x_keep.start()

    plan = {
        1: [(step_y, 0)], 3: [(step_y, 1)], 4: [(step_p, 0), (step_y, 2)], 6: [(step_p, 1)], 7: [(step_p, 2)],
    }
    for now, actions in plan.items():
        @pl.when(pl.program_id(0) == now)
        def _(actions=actions):
            for fn, w in actions:
                fn(w)

    parts = []
    inverse = []
    at = pl.multiple_of(pl.program_id(0) * rows, rows)
    for h in range(heads):
        scores = mm(qe[h, pl.ds(at, rows), :], ke[h])
        top = jnp.max(scores, axis=1, keepdims=True)
        e = jnp.exp2(scores - top).astype(BF16)
        e_ref[h] = e
        o = mm(e, ve[h])
        inv = 1.0 / o[:, HD:]
        inverse.append(inv)
        parts.append((o[:, :HD] * inv).astype(BF16))
    linv_ref[0, 0] = jnp.concatenate(inverse, axis=1)
    ctx_half[half_now] = jnp.concatenate(parts, axis=1)

    @pl.when(half_now == 1)
    def _():
        block = jnp.concatenate([ctx_half[0], ctx_half[1]], axis=1)
        ctx_ref[0] = block
        ctx_buf[t] = block
        for d in range(1, sources):
            @pl.when(t == d - 1)
            def _():
                ctx_copy(d).start()

    @pl.when(pl.program_id(0) == 2 * sources - 1)
    def _():
        ctx_own.start()
        for d in range(1, sources):
            x_copy(d).wait_send()
            r_copy(d).wait_send()
            ctx_copy(d).wait_send()
            ctx_copy(d).wait_recv()

        for d in range(1, n):
            q_copy(d).wait_send()
            v_copy(d).wait_send()
        for w in range(3):
            for d in range(1, depth):
                z_copy(w, d).wait_send()
            y_copy(w).wait_send()
            p_copy(w).wait()
        x_keep.wait()
        ctx_own.wait()


def attend(n, length, tok, wq, wo, wu, wd, vectors):
    sources, rows = GROUPS, tok.shape[0] // 2
    gw = 2 * wd.shape[1]
    heads = gw // HD
    slot = sources * 2 * rows
    depth = n // 2
    parts_q = n // GROUPS
    lanes = -(-max(v.shape[-1] for v in vectors) // 128) * 128
    block = (sources, rows, 2 * gw)
    whole = lambda *shape: pl.BlockSpec(shape, lambda s: (0,) * len(shape), pipeline_mode=pl.Buffered(1))
    out_whole = lambda *shape: pl.BlockSpec(shape, lambda s: (0,) * len(shape))
    anywhere = pl.BlockSpec(memory_space=pl.ANY)
    dma = lambda *shape: pltpu.SemaphoreType.DMA(shape)
    return pl.pallas_call(
        functools.partial(attend_kernel, n),
        grid=(2 * sources,),
        in_specs=[pl.BlockSpec(memory_space=pltpu.SMEM), whole(*tok.shape), anywhere]
        + [whole(*a.shape) for a in (wo, wu, wd) + vectors],
        out_specs=[
            pl.BlockSpec((1, rows, 2 * gw), lambda s: (s // 2, 0, 0)),
            pl.BlockSpec((1, 1, rows, gw), lambda s: (s // 2, lax.rem(s, 2), 0, 0)),
            pl.BlockSpec((heads, rows, slot), lambda s: (0, s, 0)),
            out_whole(slot, gw),
            out_whole(gw, slot),
            out_whole(gw, slot),
            out_whole(gw, 3 * gw),
            out_whole(n, 8, lanes),
            anywhere, anywhere, anywhere, anywhere, anywhere,
        ],
        out_shape=[
            jax.ShapeDtypeStruct(block, BF16),
            jax.ShapeDtypeStruct((sources, 2, rows, gw), F32),
            jax.ShapeDtypeStruct((heads, slot, slot), BF16),
            jax.ShapeDtypeStruct((slot, gw), BF16),
            jax.ShapeDtypeStruct((gw, slot), BF16),
            jax.ShapeDtypeStruct((gw, slot), BF16),
            jax.ShapeDtypeStruct((gw, 3 * gw), BF16),
            jax.ShapeDtypeStruct((n, 8, lanes), F32),
            jax.ShapeDtypeStruct(block, BF16),
            jax.ShapeDtypeStruct(block, BF16),
            jax.ShapeDtypeStruct((depth, 2) + wo.shape, BF16),
            jax.ShapeDtypeStruct((depth, 2) + wu.shape, BF16),
            jax.ShapeDtypeStruct((depth, 2) + wd.shape, BF16),
        ],
        scratch_shapes=[
            pltpu.VMEM((heads, slot, 256), BF16),
            pltpu.VMEM((heads, 256, slot), BF16),
            pltpu.VMEM((heads, slot, 128), BF16),
            pltpu.VMEM(block, BF16),
            pltpu.VMEM(block, BF16),
            pltpu.VMEM((2, rows, gw), BF16),
            pltpu.VMEM(block, BF16),
            pltpu.VMEM((n,) + wq.shape[1:], BF16),
            pltpu.VMEM((sources, parts_q) + wq.shape[1:], BF16),
            pltpu.VMEM((8, lanes), F32),
            pltpu.VMEM((n, 8, lanes), F32),
            dma(3), dma(3), dma(3), dma(3), dma(n - 1), dma(n - 1), dma(3), dma(3), dma(n - 1), dma(n - 1),
            dma(3, depth - 1), dma(3, depth - 1), dma(3), dma(3), dma(3), dma(3), dma(3), dma(6),
        ],
        compiler_params=pltpu.CompilerParams(vmem_limit_bytes=60 << 20, collective_id=1, has_side_effects=True),
        name="attend",
    )(length, tok, wq, wo, wu, wd, *vectors)


def revisit_kernel(
    n, per,
    e_ref, ctx_ref, linv_ref, qT_ref, vT_ref, k_ref, x_ref, w_ref, gctx_in, gwo_in, gwu_in, gwd_in, sm_in,
    gi_pos, gq_fin, gqv_out, gwo_out, gwu_out, gwd_out, sm_seq,
    vTe, kn, dkT, dvT, gT, gc_buf, gi_buf, sm_buf, sm_sum, gb_buf, gqv_buf, gq_buf, gq_got, gq_sum,
    mine0, mine1, mine2, core0, core1, core2, yb0, yb1, yb2, zb0, zb1, zb2, xm0, xm1, xm2, xb0, xb1, xb2, f0, f1, f2,
    g_send, g_recv, i_send, i_recv, sm_send, sm_recv, ss_send, ss_recv, b_send, b_recv, bs_send, bs_recv,
    q_send, q_recv, qs_send, qs_recv, c_send, c_recv, y_send, y_recv, z_send, z_recv, xs_send, xs_recv, p_send, p_recv, own, local,
):
    heads = kn.shape[0]
    sources, rows, _ = x_ref.shape
    gw = heads * HD
    slot = sources * 2 * rows
    parts_q = n // GROUPS
    u = pl.program_id(0)
    now = 2 * GROUPS - 1 - u
    half_now = lax.rem(now, 2)
    j = now // 2
    i = lax.axis_index("dp")
    me = lax.axis_index("seq")
    c = lax.rem(me, 2)
    y = lax.rem(i, 2)
    k = i // 2
    depth = n // 2
    across = lax.rem(me + 2, sources)
    every = slice(None)
    inputs = (gwo_in, gwu_in, gwd_in)
    outputs = (gwo_out, gwu_out, gwd_out)
    mine, core, ybuf, zbuf = (mine0, mine1, mine2), (core0, core1, core2), (yb0, yb1, yb2), (zb0, zb1, zb2)
    xmine, xbuf, final = (xm0, xm1, xm2), (xb0, xb1, xb2), (f0, f1, f2)

    def g_copy(d):
        peer = lax.rem(me + d, sources)
        return remote(gctx_in.at[peer], gc_buf.at[sources - 1 - d], g_send.at[d - 1], g_recv.at[d - 1], i, peer)

    def i_copy(d):
        return remote(gi_buf.at[d - 1], gi_pos.at[me], i_send.at[d - 1], i_recv.at[d - 1], i, lax.rem(me + d, sources))

    def sm_copy(d):
        to = lax.rem(i + d, n)
        return remote(sm_in.at[to], sm_buf.at[d - 1], sm_send.at[d - 1], sm_recv.at[d - 1], to, me)

    def ss_copy(d):
        return remote(sm_sum, sm_seq.at[me], ss_send.at[d - 1], ss_recv.at[d - 1], i, lax.rem(me + d, sources))

    def b_copy(d):
        return remote(gb_buf.at[i], gb_buf.at[i], b_send.at[d - 1], b_recv.at[d - 1], lax.rem(i + d, n), me)

    def bs_copy(d):
        return remote(gqv_buf, gqv_out, bs_send.at[d - 1], bs_recv, i, lax.rem(me + d, sources))

    def q_copy(d):
        to = lax.rem(i + d, n)
        return remote(gq_buf.at[to], gq_got.at[d - 1], q_send.at[d - 1], q_recv.at[d - 1], to, me)

    def qs_copy(d):
        spot = lax.rem(i, GROUPS)
        return remote(
            gq_sum, gq_fin.at[spot], qs_send.at[d], qs_recv.at[spot], me * parts_q + i // GROUPS, lax.rem(me + d, sources)
        )

    def own_copy(w):
        return pltpu.make_async_copy(half_of(inputs[w], (every, every), c), mine[w], own.at[w])

    def c_copy(w):
        return remote(half_of(inputs[w], (every, every), 1 - c), core[w], c_send.at[w], c_recv.at[w], i, other(me))

    def y_copy(w):
        return remote(mine[w].at[:, 1 - y], ybuf[w], y_send.at[w], y_recv.at[w], other(i), me)

    def z_copy(w, d):
        to = lax.rem(k + d, depth)
        return remote(mine[w].at[to, y], zbuf[w].at[d - 1], z_send.at[w, d - 1], z_recv.at[w, d - 1], to * 2 + y, me)

    def x_copy(w):
        return remote(xmine[w], xbuf[w], xs_send.at[w], xs_recv.at[w], i, across)

    def p_copy(w):
        return remote(final[w], outputs[w].at[c], p_send.at[w], p_recv.at[w], i, other(me))

    g_own = pltpu.make_async_copy(gctx_in.at[me], gc_buf.at[sources - 1], local.at[0])
    sm_own = pltpu.make_async_copy(sm_in.at[i], sm_buf.at[n - 1], local.at[1])
    ss_own = pltpu.make_async_copy(sm_sum, sm_seq.at[me], local.at[2])
    bs_own = pltpu.make_async_copy(gqv_buf, gqv_out, local.at[3])
    qs_own = pltpu.make_async_copy(gq_sum, gq_fin.at[lax.rem(i, GROUPS)], local.at[4])
    i_own = pltpu.make_async_copy(gi_buf.at[sources - 1], gi_pos.at[me], local.at[5])

    def p_own(w):
        return pltpu.make_async_copy(final[w], outputs[w].at[c], local.at[6 + w])

    stays = me * parts_q + i // GROUPS == i
    count = gw // per
    bias_owner = lax.rem(i // count, GROUPS) == me

    def step_y(w):
        own_copy(w).wait()
        c_copy(w).wait_recv()
        mine[w][...] += core[w][...]
        y_copy(w).start()

    def step_z(w):
        y_copy(w).wait_recv()
        mine[w][:, y] += ybuf[w][...]
        for d in range(1, depth):
            z_copy(w, d).start()

    def step_x(w):
        total = mine[w][k, y].astype(F32)
        for d in range(1, depth):
            z_copy(w, d).wait_recv()
            total += zbuf[w][d - 1].astype(F32)
        xmine[w][...] = total.astype(BF16)
        x_copy(w).start()

    def step_p(w):
        x_copy(w).wait_recv()
        final[w][...] = xmine[w][...].astype(F32) + xbuf[w][...].astype(F32)
        p_copy(w).start()
        p_own(w).start()

    def small_sum():
        sm_own.wait()
        total = sm_buf[n - 1]
        for d in range(1, n):
            sm_copy(d).wait_recv()
            total += sm_buf[d - 1]
        sm_sum[...] = total
        ss_own.start()
        for d in range(1, sources):
            ss_copy(d).start()

    @pl.when(u == 0)
    def _():
        greet(n, sources, i, me)
        for d in (1, 2, 3):
            g_copy(d).start()
        g_own.start()
        for w in range(3):
            c_copy(w).start()
            own_copy(w).start()
        sm_own.start()
        for d in range(1, n):
            sm_copy(d).start()
        dkT[...] = jnp.zeros_like(dkT)
        dvT[...] = jnp.zeros_like(dvT)
        row = lax.broadcasted_iota(jnp.int32, (HD, slot), 0)
        ones_rows = jnp.where(row < 2, 1.0, 0.0).astype(BF16)
        for h in range(heads):
            cols = slice(h * HD, (h + 1) * HD)
            vTe[h, 0:HD, :] = vT_ref[cols, :]
            vTe[h, HD:, :] = ones_rows
            kn[h] = k_ref[:, cols]
        g_own.wait()

    for d in range(1, sources):
        @pl.when(u == 2 * d)
        def _(d=d):
            g_copy(d).wait_recv()

    plan = {
        1: [(step_y, 0), (step_y, 1)], 2: [(step_y, 2)], 3: [(step_z, 0)], 5: [(step_z, 1)], 6: [(step_x, 0)],
        7: [(step_z, 2), (step_x, 1), (step_p, 0)],
    }
    for when_u, actions in plan.items():
        @pl.when(u == when_u)
        def _(actions=actions):
            for fn, w in actions:
                fn(w)

    @pl.when(u == 4)
    def _():
        small_sum()

    lane = lax.broadcasted_iota(jnp.int32, (rows, HD), 1)
    at = pl.multiple_of(now * rows, rows)
    both = gc_buf[j].astype(F32)
    g = jnp.where(half_now == 0, both[:, :gw], both[:, gw:]) * linv_ref[0, 0]
    g_low = g.astype(BF16)
    gT_low = g_low.T
    both = ctx_ref[0].astype(F32)
    prod = g * jnp.where(half_now == 0, both[:, :gw], both[:, gw:])
    dqs = []
    for h in range(heads):
        cols = slice(h * HD, (h + 1) * HD)
        delta = -jnp.sum(prod[:, cols], axis=1, keepdims=True)
        d_hi = delta.astype(BF16)
        d_lo = (delta - d_hi.astype(F32)).astype(BF16)
        tail = jnp.where(lane == 0, d_hi, jnp.where(lane == 1, d_lo, jnp.zeros((), BF16)))
        ge = jnp.concatenate([g_low[:, cols], tail], axis=1)
        e = e_ref[h]
        ds = (e.astype(F32) * mm(ge, vTe[h])).astype(BF16)
        dvT[cols, :] += mm(gT_low[cols, :], e)
        dkT[cols, :] += mm(qT_ref[cols, :], ds)
        dqs.append((mm(ds, kn[h]) * (HD ** (-0.5))).astype(BF16))
    gT[0:gw, pl.ds(at, rows)] = jnp.concatenate(dqs, axis=1).T

    @pl.when(u == 2 * sources - 1)
    def _():
        gT[gw : 2 * gw, :] = (dkT[...] * (HD ** (-0.5))).astype(BF16)
        gT[2 * gw :, :] = dvT[...].astype(BF16)
        sums = [None, None]
        for q in range(sources):
            for half in range(2):
                part = mm(gT[:, (q * 2 + half) * rows : (q * 2 + half + 1) * rows], x_ref[q, :, window(half)])
                sums[half] = part if sums[half] is None else sums[half] + part
        gq = (sums[0][:, :gw] + sums[1][:, 64:]).T
        size = gw // n
        for piece in range(n):
            gq_buf[piece] = gq[piece * size : (piece + 1) * size].astype(BF16)
        gb_buf[i] = mm_nt(jnp.ones((8, slot), BF16), gT[...])
        ready = 0
        for q in (1, 0, 2, 3):
            packed = [
                mm(w_ref[...], gT[:, (q * 2 + half) * rows : (q * 2 + half + 1) * rows]).T.astype(BF16)
                for half in range(2)
            ]
            block = jnp.concatenate(packed, axis=1)
            if ready:
                i_copy(ready).start()
            else:
                for d in range(1, n):
                    q_copy(d).start()
                for d in range(1, n):
                    b_copy(d).start()
            gi_buf[q] = block
            ready = q + 1
        i_own.start()
        step_x(2)
        step_p(1)
        total = gq_buf[i].astype(F32)
        for d in range(1, n):
            q_copy(d).wait_recv()
            total += gq_got[d - 1].astype(F32)
        gq_sum[...] = total.astype(BF16)
        for d in range(1, n):
            b_copy(d).wait_recv()

        @pl.when(bias_owner)
        def _():
            total = gb_buf[0, 0:1, :]
            for d in range(1, n):
                total += gb_buf[d, 0:1, :]
            side = jnp.where(i < n // 2, total[:, :gw], total[:, 2 * gw :])
            piece = lax.rem(i, count)
            value = side[:, 0:per]
            for v in range(1, count):
                value = jnp.where(piece == v, side[:, v * per : (v + 1) * per], value)
            gqv_buf[0:1, 0:per] = value
            bs_own.start()
            for d in range(1, sources):
                bs_copy(d).start()

        for d in range(1, sources):
            qs_copy(d).start()

        @pl.when(stays)
        def _():
            qs_own.start()

        @pl.when(jnp.logical_not(stays))
        def _():
            qs_copy(0).start()

        step_p(2)

        ss_own.wait()
        i_own.wait()
        for d in range(1, sources):
            ss_copy(d).wait_recv()
            i_copy(d).wait_recv()
        for w in range(3):
            p_copy(w).wait_recv()
            p_own(w).wait()

        @pl.when(jnp.logical_not(bias_owner))
        def _():
            bs_copy(1).wait_recv()

        for spot in range(GROUPS):
            source = lax.rem(i, parts_q) * GROUPS + spot

            @pl.when(jnp.logical_not(jnp.logical_and(i // parts_q == me, source == i)))
            def _():
                remote(gq_sum, gq_fin.at[spot], qs_send.at[0], qs_recv.at[spot], other(i), me).wait_recv()

        for d in range(1, sources):
            g_copy(d).wait_send()
            i_copy(d).wait_send()
            ss_copy(d).wait_send()

        @pl.when(bias_owner)
        def _():
            bs_own.wait()
            for d in range(1, sources):
                bs_copy(d).wait_send()

        for d in range(1, sources):
            qs_copy(d).wait_send()

        @pl.when(stays)
        def _():
            qs_own.wait()

        @pl.when(jnp.logical_not(stays))
        def _():
            qs_copy(0).wait_send()

        for d in range(1, n):
            q_copy(d).wait_send()
        for d in range(1, n):
            sm_copy(d).wait_send()
            b_copy(d).wait_send()
        for w in range(3):
            c_copy(w).wait_send()
            y_copy(w).wait_send()
            for d in range(1, depth):
                z_copy(w, d).wait_send()
            x_copy(w).wait_send()
            p_copy(w).wait_send()


def revisit(n, per, e, ctx, linv, qT, vT, k, x, w, gctx, gwo, gwu, gwd, small):
    sources, rows, _ = x.shape
    gw = w.shape[0]
    heads = gw // HD
    slot = sources * 2 * rows
    depth = n // 2
    last = 2 * sources - 1
    whole = lambda *shape: pl.BlockSpec(shape, lambda s: (0,) * len(shape), pipeline_mode=pl.Buffered(1))
    anywhere = pl.BlockSpec(memory_space=pl.ANY)
    dma = lambda *shape: pltpu.SemaphoreType.DMA(shape)

    def half_shape(a):
        return a.shape[3:] if len(a.shape) == 5 else (a.shape[2], a.shape[3] // 2)

    halves = [half_shape(a) for a in (gwo, gwu, gwd)]
    outs = [
        jax.ShapeDtypeStruct(x.shape, BF16),
        jax.ShapeDtypeStruct((GROUPS, gw // n, 3 * gw), BF16),
        jax.ShapeDtypeStruct((8, 256), F32),
        jax.ShapeDtypeStruct((2,) + halves[0], F32),
        jax.ShapeDtypeStruct((2,) + halves[1], F32),
        jax.ShapeDtypeStruct((2,) + halves[2], F32),
        jax.ShapeDtypeStruct((sources,) + small.shape[1:], F32),
    ]
    vmem = pltpu.VMEM
    return pl.pallas_call(
        functools.partial(revisit_kernel, n, per),
        grid=(2 * sources,),
        in_specs=[
            pl.BlockSpec((heads, rows, slot), lambda s: (0, last - s, 0)),
            pl.BlockSpec((1, rows, 2 * gw), lambda s: ((last - s) // 2, 0, 0)),
            pl.BlockSpec((1, 1, rows, gw), lambda s: ((last - s) // 2, lax.rem(last - s, 2), 0, 0)),
            pl.BlockSpec((gw, rows), lambda s: (0, last - s)),
            whole(*vT.shape), whole(*k.shape), whole(*x.shape), whole(*w.shape),
            anywhere, anywhere, anywhere, anywhere, anywhere,
        ],
        out_specs=[anywhere] * len(outs),
        out_shape=outs,
        scratch_shapes=[
            vmem((heads, 2 * HD, slot), BF16),
            vmem((heads, slot, HD), BF16),
            vmem((gw, slot), F32),
            vmem((gw, slot), F32),
            vmem((3 * gw, slot), BF16),
            vmem(x.shape, BF16), vmem(x.shape, BF16),
            vmem(small.shape, F32), vmem(small.shape[1:], F32),
            vmem((n, 8, 3 * gw), F32), vmem((8, 256), F32),
            vmem((n, gw // n, 3 * gw), BF16),
            vmem((n - 1, gw // n, 3 * gw), BF16),
            vmem((gw // n, 3 * gw), BF16),
        ]
        + [vmem((depth, 2) + s, BF16) for s in halves]
        + [vmem((depth, 2) + s, BF16) for s in halves]
        + [vmem((depth,) + s, BF16) for s in halves]
        + [vmem((depth - 1,) + s, BF16) for s in halves]
        + [vmem(s, BF16) for s in halves]
        + [vmem(s, BF16) for s in halves]
        + [vmem(s, F32) for s in halves]
        + [
            dma(3), dma(3), dma(3), dma(3), dma(n - 1), dma(n - 1), dma(3), dma(3), dma(n - 1), dma(n - 1),
            dma(3), pltpu.SemaphoreType.DMA, dma(n - 1), dma(n - 1), dma(4), dma(4),
            dma(3), dma(3), dma(3), dma(3), dma(3, depth - 1), dma(3, depth - 1), dma(3), dma(3), dma(3), dma(3), dma(3), dma(9),
        ],
        compiler_params=pltpu.CompilerParams(vmem_limit_bytes=62 << 20, collective_id=2, has_side_effects=True),
        name="revisit",
    )(e, ctx, linv, qT, vT, k, x, w, gctx, gwo, gwu, gwd, small)


def split_rows(values):
    mean = jnp.mean(values, axis=-1, keepdims=True)
    centred = values - mean
    var = jnp.mean(centred * centred, axis=-1, keepdims=True)
    return centred, lax.rsqrt(var + epsilon)


def norm_back(grad, unit, inverse, gain):
    g = grad * gain
    m1 = jnp.mean(g, axis=-1, keepdims=True)
    m2 = jnp.mean(g * unit, axis=-1, keepdims=True)
    return inverse * (g - m1 - unit * m2)


def join_windows(parts):
    tiles = []
    for even, odd in zip(parts[0::2], parts[1::2]):
        tiles += [even[:, :128], even[:, 128:] + odd[:, :128], odd[:, 128:]]
    return jnp.concatenate(tiles, axis=1)


def group_window(g):
    at = (g // 2) * 384 + (g % 2) * 128
    return slice(at, at + 256)


def middle_kernel(
    n, len_ref, ctx_ref, tok_ref, gout_ref, wo_ref, wu_ref, wd_ref, vec_ref,
    out_ref, gctx_ref, gres_ref, gwo_ref, gwu_ref, gwd_ref, small_ref, upad, dpad, awo, awu, awd, sums, usums,
):
    rows = ctx_ref.shape[1]
    gw = ctx_ref.shape[2] // 2
    width = tok_ref.shape[1]
    hidden = wu_ref.shape[1]
    share = width // n
    first_row = lax.axis_index("seq") * (2 * rows)
    vec = join_lanes([vec_ref[d, :, 0:share] for d in range(n)])
    obias, gain1, shift1, dbias, gain2, shift2 = (vec[v : v + 1] for v in range(1, 7))
    count = n // GROUPS
    for g in range(GROUPS):
        upad[g] = pad_rows(wu_ref[g * gw : (g + 1) * gw, :], g % 2)
        odd = 64 * (g % 2)
        dpad[g, 192 * (1 - g % 2) : 192 * (1 - g % 2) + 64, :] = jnp.zeros((64, hidden), BF16)
        size = hidden // count
        for d in range(count):
            for v in range(2):
                at = odd + v * (gw // 2)
                dpad[g, at : at + gw // 2, d * size : (d + 1) * size] = wd_ref[g * count + d, v]
    packed = [[] for _ in range(GROUPS)]
    for half in range(2):
        first = half == 0

        def keep(ref, at, value):
            if first:
                ref[at] = value
            else:
                ref[at] += value

        r = slice(half * rows, (half + 1) * rows)
        x = tok_ref[r, :].astype(F32) + obias
        for g in range(GROUPS):
            x += mm(ctx_ref[g, :, window(half)], pad_rows(wo_ref[g * gw : (g + 1) * gw, :], half))
        c1, i1 = split_rows(x)
        n1 = c1 * i1
        mixed = n1 * gain1 + shift1
        low = mixed.astype(BF16)
        lowered = []
        slopes = []
        actives = []
        for g in range(GROUPS):
            ub = join_lanes([vec_ref[g * count + d, 7:8, 0 : hidden // count] for d in range(count)])
            u = mm(low[:, group_window(g)], upad[g]) + ub
            phi = 0.5 + 0.5 * lax.erf(u * (0.5 ** 0.5))
            slope = phi + u * (jnp.exp(u * u * -0.5) * 0.3989422804014327)
            act = (u * phi).astype(BF16)
            actives.append(act)
            slopes.append(slope)
            lowered.append(mm_nt(act, dpad[g]))
        x = mixed + join_windows(lowered) + dbias
        c2, i2 = split_rows(x)
        n2 = c2 * i2
        row = lax.broadcasted_iota(jnp.int32, (rows, 1), 0) + (first_row + half * rows)
        valid = jnp.where(row < len_ref[0], 1.0, 0.0)
        out_ref[r, :] = (valid * (n2 * gain2 + shift2)).astype(BF16)
        gy = gout_ref[r, :].astype(F32) * valid
        d2 = norm_back(gy, n2, i2, gain2)
        keep(sums, slice(4, 5), jnp.sum(gy * n2, axis=0, keepdims=True))
        keep(sums, slice(5, 6), jnp.sum(gy, axis=0, keepdims=True))
        keep(sums, slice(3, 4), jnp.sum(d2, axis=0, keepdims=True))
        d2_low = d2.astype(BF16)
        backs = []
        for g in range(GROUPS):
            win = d2_low[:, group_window(g)]
            odd = 64 * (g % 2)
            part = mm_tn(win, actives[g])[odd : odd + gw]
            if first:
                awd[g] = part
            else:
                part = (awd[g] + part).astype(BF16)
                size = hidden // count
                for d in range(count):
                    for v in range(2):
                        gwd_ref[g * count + d, v] = part[v * (gw // 2) : (v + 1) * (gw // 2), d * size : (d + 1) * size]
            gu = mm(win, dpad[g]) * slopes[g]
            keep(usums, slice(g, g + 1), jnp.sum(gu, axis=0, keepdims=True))
            gu_low = gu.astype(BF16)
            part = mm_tn(low[:, group_window(g)], gu_low)[odd : odd + gw]
            if first:
                awu[g] = part
            else:
                gwu_ref[g * gw : (g + 1) * gw, :] = (awu[g] + part).astype(BF16)
            backs.append(mm_nt(gu_low, upad[g]))
        gm = join_windows(backs) + d2
        d1 = norm_back(gm, n1, i1, gain1)
        keep(sums, slice(1, 2), jnp.sum(gm * n1, axis=0, keepdims=True))
        keep(sums, slice(2, 3), jnp.sum(gm, axis=0, keepdims=True))
        keep(sums, slice(0, 1), jnp.sum(d1, axis=0, keepdims=True))
        gres_ref[r, :] = d1
        d1_low = d1.astype(BF16)
        for g in range(GROUPS):
            part = mm_tn(ctx_ref[g, :, window(half)], d1_low)[64 * half : 64 * half + gw]
            if first:
                awo[g] = part
            else:
                gwo_ref[g * gw : (g + 1) * gw, :] = (awo[g] + part).astype(BF16)
        back = mm_nt(d1_low, wo_ref[...]).astype(BF16)
        for g in range(GROUPS):
            packed[g].append(back[:, g * gw : (g + 1) * gw])
    for g in range(GROUPS):
        gctx_ref[g] = jnp.concatenate(packed[g], axis=1)
    sums[6:8, :] = jnp.zeros((2, width), F32)
    up_share = hidden // count
    for d in range(n):
        small_ref[d] = jnp.zeros(small_ref.shape[1:], F32)
        small_ref[d, 0:8, 0:share] = sums[0:8, d * share : (d + 1) * share]
        at = (d % count) * up_share
        for v in range(0, up_share, 128):
            size = min(128, up_share - v)
            small_ref[d, 8 + v // 128 : 9 + v // 128, 0:size] = usums[d // count : d // count + 1, at + v : at + v + size]


def middle(n, length, ctx, tok, gout, wo, wu, wd, vec):
    hidden = wu.shape[1]
    width = tok.shape[1]
    gw = width // GROUPS
    vmem = pl.BlockSpec(memory_space=pltpu.VMEM)
    return pl.pallas_call(
        functools.partial(middle_kernel, n),
        in_specs=[pl.BlockSpec(memory_space=pltpu.SMEM)] + [vmem] * 7,
        out_specs=[vmem] * 7,
        out_shape=[
            jax.ShapeDtypeStruct(tok.shape, BF16),
            jax.ShapeDtypeStruct(ctx.shape, BF16),
            jax.ShapeDtypeStruct(tok.shape, F32),
            jax.ShapeDtypeStruct(wo.shape, BF16),
            jax.ShapeDtypeStruct(wu.shape, BF16),
            jax.ShapeDtypeStruct(wd.shape, BF16),
            jax.ShapeDtypeStruct((n, 16, 128), F32),
        ],
        scratch_shapes=[
            pltpu.VMEM((GROUPS, 256, hidden), BF16),
            pltpu.VMEM((GROUPS, 256, hidden), BF16),
            pltpu.VMEM((GROUPS, gw, width), F32),
            pltpu.VMEM((GROUPS, gw, hidden), F32),
            pltpu.VMEM((GROUPS, gw, hidden), F32),
            pltpu.VMEM((8, width), F32),
            pltpu.VMEM((8, hidden), F32),
        ],
        compiler_params=pltpu.CompilerParams(vmem_limit_bytes=62 << 20),
        name="middle",
    )(length, ctx, tok, gout, wo, wu, wd, vec)


def finish_kernel(
    gi_ref, gres_ref, gq_ref, gqv_ref, gwo_ref, gwu_ref, gwd_ref, sm_ref,
    tok_out, qkv_out, qv_out, wo_out, b0_out, b1_out, b2_out, wu_out, up_out, wd_out, b3_out, b4_out, b5_out,
):
    rows = gi_ref.shape[1]
    gw = gi_ref.shape[2] // 2
    for half in range(2):
        r = slice(half * rows, (half + 1) * rows)
        lanes = slice(half * gw, (half + 1) * gw)
        for pair in range(GROUPS // 2):
            both = jnp.concatenate([gi_ref[2 * pair, :, lanes], gi_ref[2 * pair + 1, :, lanes]], axis=1)
            wide = slice(pair * 2 * gw, (pair + 1) * 2 * gw)
            tok_out[r, wide] = (both.astype(F32) + gres_ref[r, wide]).astype(BF16)
    qkv_out[...] = jnp.concatenate([gq_ref[v].astype(F32) for v in range(gq_ref.shape[0])], axis=0)
    qv_out[...] = gqv_ref[0:1, 0 : qv_out.shape[1]]
    for ref, out in ((gwo_ref, wo_out), (gwu_ref, wu_out)):
        out[...] = jnp.concatenate([ref[0], ref[1]], axis=1)
    size = gwd_ref.shape[1]
    for v in range(2):
        wd_out[v * size : (v + 1) * size, :] = gwd_ref[v]
    total = sm_ref[0] + sm_ref[1] + sm_ref[2] + sm_ref[3]
    for v, out in enumerate((b0_out, b1_out, b2_out, b3_out, b4_out, b5_out)):
        out[...] = total[v : v + 1, 0 : out.shape[1]]
    for v in range(0, up_out.shape[1], 128):
        step = min(128, up_out.shape[1] - v)
        up_out[:, v : v + step] = total[8 + v // 128 : 9 + v // 128, 0:step]


def finish(shapes, *args):
    vmem = pl.BlockSpec(memory_space=pltpu.VMEM)
    return pl.pallas_call(
        finish_kernel,
        in_specs=[vmem] * len(args),
        out_specs=[vmem] * len(shapes),
        out_shape=[jax.ShapeDtypeStruct(s, BF16 if v == 0 else F32) for v, s in enumerate(shapes)],
        compiler_params=pltpu.CompilerParams(vmem_limit_bytes=60 << 20),
        name="finish",
    )(*args)


def on_device(
    tokens, lengths, qkv_weight, qv_bias, out_weight, out_bias, norm_gain, norm_shift,
    up_weight, up_bias, down_weight, down_bias, final_gain, final_shift, grad_output,
):
    n = lax.axis_size("dp")
    width = tokens.shape[2]
    per = qv_bias.shape[0]
    vectors = tuple(
        a[None] if a.shape[0] <= 128 else a for a in (qv_bias, out_bias, norm_gain, norm_shift, down_bias, final_gain, final_shift, up_bias)
    )
    wq = qkv_weight.reshape(GROUPS, qkv_weight.shape[0] // GROUPS, qkv_weight.shape[1])
    wd_halves = down_weight.T.reshape(2, down_weight.shape[1] // 2, down_weight.shape[0])
    ctx, linv, e, k, qT, vT, w, vecs, x_all, ctx_pos, wo, wu, wd = attend(
        n, lengths, tokens[0], wq, out_weight, up_weight, wd_halves, vectors
    )
    output, gctx, gres, gwo, gwu, gwd, small = middle(
        n, lengths, ctx_pos, tokens[0], grad_output[0],
        wo.reshape(width, width), wu.reshape(width, -1), wd.reshape((n,) + wd.shape[2:]), vecs,
    )
    parts = revisit(
        n, per, e, ctx, linv, qT, vT, k, x_all, w, gctx,
        gwo.reshape(wo.shape), gwu.reshape(wu.shape), gwd.reshape(wd.shape), small,
    )
    one = lambda a: (1, a.shape[0])
    shapes = (
        tokens.shape[1:], qkv_weight.shape, one(qv_bias), out_weight.shape, one(out_bias), one(norm_gain),
        one(norm_shift), up_weight.shape, one(up_bias), down_weight.shape[::-1], one(down_bias), one(final_gain), one(final_shift),
    )
    outs = list(finish(shapes, parts[0], gres, *parts[1:]))
    outs[9] = outs[9].T
    flat = [a[0] if a.shape[0] == 1 else a for a in outs[1:]]
    return (output[None], outs[0][None], *flat)


def solution(mesh):
    rows = P("dp", "seq", None)
    mat = P("dp", None)
    vec = P("dp")
    in_specs = (rows, vec, mat, vec, mat, vec, vec, vec, mat, vec, mat, vec, vec, vec, rows)
    out_specs = (rows, rows, mat, vec, mat, vec, vec, vec, mat, vec, mat, vec, vec, vec)
    return jax.shard_map(on_device, mesh=mesh, in_specs=in_specs, out_specs=out_specs, check_vma=False)
```

time: 173 us -> 138 us (0.80); the launches traced: 170 us -> 138 us
  local copies, waits for them, and re-layouts: 19.4 us -> 0 us
  Pallas kernels: 148 us -> 135 us
    pallas_call x2 -> x3, Pallas kernels: 130 us -> 117 us  [the longest x1 59.3 us: revisit(): pl.pallas_call(functools.partial(revisit_kernel, n, per), grid=(2 * sourc...]
    unnamed x16 -> x0, local copies, waits for them, and re-layouts: 9.8 us -> none
    pad x7 -> x0, local copies, waits for them, and re-layouts: 4.62 us -> none  [on_device(): jnp.pad(a.astype(F32), (0, lanes - a.shape[0]))]
where the time goes in v3:
time: 138 us
  Pallas kernels  135 us (98%)
    pallas_call x1, Pallas kernels, revisit(): pl.pallas_call(functools.partial(revisit_kernel, n, per), grid=(2 * sourc...  59.3 us
    pallas_call x1, Pallas kernels, attend(): pl.pallas_call(functools.partial(attend_kernel, n), grid=(2 * sources,),...  54.6 us
    pallas_call x1, Pallas kernels, middle(): pl.pallas_call(functools.partial(middle_kernel, n), in_specs=[pl.BlockSpe...  18 us
    pallas_call x1, Pallas kernels, finish(): pl.pallas_call(finish_kernel, in_specs=[vmem] * len(args), out_specs=[vme...  3.39 us

profile of v3, /device:TPU:0, one launch (start us, length us, event | category | flops | bytes accessed | tf_op | source)
XLA Modules:
  0.0 137.9 jit_solution(10741631625778244389)
XLA Ops:
  1.3 54.6 %attend.1 = (bf16[4,256,384]{2,1,0:T(8,128)(2,1)}, f32[4,2,256,192]{3,2,1,0:T(8,128)}, bf16[3,2048,2048]{2,1,0:T(8,128)(2,1)}, bf16[2048,192]{1,0:T(8,128)(2,1)}...) custom-call(s32[1]{0:T(128)S(6)} %copy.29.len_ref, ...), custom_call_target="tpu_custom_call" | custom-call | tf_op jit(solution)/shard_map/attend/pallas_call | solution.py:335
  55.9 18.0 %middle.1 = (bf16[512,768]{1,0:T(8,128)(2,1)}, bf16[4,256,384]{2,1,0:T(8,128)(2,1)}, f32[512,768]{1,0:T(8,128)}, bf16[768,768]{1,0:T(8,128)(2,1)}, bf16[768,768]...) custom-call(s32[1]{0:T(128)S(6)} %copy.29.len_ref, ...), custom_call_target="tpu_custom_call" | custom-call | tf_op jit(solution)/shard_map/middle/pallas_call | solution.py:921
  74.0 59.3 %revisit.1 = (bf16[4,256,384]{2,1,0:T(8,128)(2,1)}, bf16[4,24,576]{2,1,0:T(8,128)(2,1)}, f32[8,256]{1,0:T(8,128)}, f32[2,96,384]{2,1,0:T(8,128)}, f32[2,96,384]{...) custom-call(bf16[3,2048,2048]{2,1,0:T(8,128)(2,1)} %get-tuple-element.60.e_ref, ...), custom_call_target="tpu_custom_call" | custom-call | tf_op jit(solution)/shard_map/revisit/pallas_call | solution.py:732
  133.2 3.4 %finish.1 = (bf16[512,768]{1,0:T(8,128)(2,1)}, f32[96,576]{1,0:T(8,128)}, f32[1,192]{1,0:T(1,128)}, f32[96,768]{1,0:T(8,128)}, f32[1,96]{1,0:T(1,128)}, /*index=...) custom-call(bf16[4,256,384]{2,1,0:T(8,128)(2,1)} %get-tuple-element., ...), custom_call_target="tpu_custom_call" | custom-call | tf_op jit(solution)/shard_map/finish/pallas_call | solution.py:978
  136.6 1.3 reduce

commit v4 on v3

--- a/solution.py
+++ b/solution.py
@@ -190,10 +190,6 @@
         v_own.start()
         for d in range(1, n):
             v_copy(d).start()
-        for w in range(3):
-            for d in range(1, depth):
-                z_copy(w, d).start()
-            own_copy(w).start()
 
         scale = HD ** (-0.5) * LOG2E
         lane = lax.broadcasted_iota(jnp.int32, (slot, 128), 1)
@@ -213,6 +209,10 @@
             q_copy(d).wait_recv()
         for d in range(1, sources):
             r_copy(d).start()
+        for w in range(3):
+            for d in range(1, depth):
+                z_copy(w, d).start()
+            own_copy(w).start()
 
         @pl.when(c == 0)
         def _():
@@ -265,7 +265,7 @@
         x_keep.start()
 
     plan = {
-        1: [(step_y, 0)], 3: [(step_y, 1)], 4: [(step_p, 0), (step_y, 2)], 6: [(step_p, 1)], 7: [(step_p, 2)],
+        0: [(step_y, 0)], 1: [(step_y, 1)], 3: [(step_p, 0), (step_y, 2)], 5: [(step_p, 1)], 7: [(step_p, 2)],
     }
     for now, actions in plan.items():
         @pl.when(pl.program_id(0) == now)

time: 138 us -> 135 us (0.978)
  Pallas kernels: 135 us -> 131 us
    pallas_call x1, Pallas kernels: 59.3 us -> 55.5 us  [revisit(): pl.pallas_call(functools.partial(revisit_kernel, n, per), grid=(2 * sourc...]
where the time goes in v4:
time: 135 us; the launch traced here: 134 us
  Pallas kernels  131 us (97%)
    pallas_call x1, Pallas kernels, revisit(): pl.pallas_call(functools.partial(revisit_kernel, n, per), grid=(2 * sourc...  55.5 us
    pallas_call x1, Pallas kernels, attend(): pl.pallas_call(functools.partial(attend_kernel, n), grid=(2 * sources,),...  54.3 us
    pallas_call x1, Pallas kernels, middle(): pl.pallas_call(functools.partial(middle_kernel, n), in_specs=[pl.BlockSpe...  18 us
    pallas_call x1, Pallas kernels, finish(): pl.pallas_call(finish_kernel, in_specs=[vmem] * len(args), out_specs=[vme...  3.39 us

profile of v4, /device:TPU:0, one launch (start us, length us, event | category | flops | bytes accessed | tf_op | source)
XLA Modules:
  0.0 133.8 jit_solution(9975648001856740940)
XLA Ops:
  1.3 54.3 %attend.1 = (bf16[4,256,384]{2,1,0:T(8,128)(2,1)}, f32[4,2,256,192]{3,2,1,0:T(8,128)}, bf16[3,2048,2048]{2,1,0:T(8,128)(2,1)}, bf16[2048,192]{1,0:T(8,128)(2,1)}...) custom-call(s32[1]{0:T(128)S(6)} %copy.29.len_ref, ...), custom_call_target="tpu_custom_call" | custom-call | tf_op jit(solution)/shard_map/attend/pallas_call | solution.py:335
  55.6 18.0 %middle.1 = (bf16[512,768]{1,0:T(8,128)(2,1)}, bf16[4,256,384]{2,1,0:T(8,128)(2,1)}, f32[512,768]{1,0:T(8,128)}, bf16[768,768]{1,0:T(8,128)(2,1)}, bf16[768,768]...) custom-call(s32[1]{0:T(128)S(6)} %copy.29.len_ref, ...), custom_call_target="tpu_custom_call" | custom-call | tf_op jit(solution)/shard_map/middle/pallas_call | solution.py:921
  73.6 55.5 %revisit.1 = (bf16[4,256,384]{2,1,0:T(8,128)(2,1)}, bf16[4,24,576]{2,1,0:T(8,128)(2,1)}, f32[8,256]{1,0:T(8,128)}, f32[2,96,384]{2,1,0:T(8,128)}, f32[2,96,384]{...) custom-call(bf16[3,2048,2048]{2,1,0:T(8,128)(2,1)} %get-tuple-element.60.e_ref, ...), custom_call_target="tpu_custom_call" | custom-call | tf_op jit(solution)/shard_map/revisit/pallas_call | solution.py:732
  129.2 3.4 %finish.1 = (bf16[512,768]{1,0:T(8,128)(2,1)}, f32[96,576]{1,0:T(8,128)}, f32[1,192]{1,0:T(1,128)}, f32[96,768]{1,0:T(8,128)}, f32[1,96]{1,0:T(1,128)}, /*index=...) custom-call(bf16[4,256,384]{2,1,0:T(8,128)(2,1)} %get-tuple-element., ...), custom_call_target="tpu_custom_call" | custom-call | tf_op jit(solution)/shard_map/finish/pallas_call | solution.py:978
  132.6 1.3 reduce

commit v5 on v4

--- a/solution.py
+++ b/solution.py
@@ -959,7 +959,7 @@
             wide = slice(pair * 2 * gw, (pair + 1) * 2 * gw)
             tok_out[r, wide] = (both.astype(F32) + gres_ref[r, wide]).astype(BF16)
     qkv_out[...] = jnp.concatenate([gq_ref[v].astype(F32) for v in range(gq_ref.shape[0])], axis=0)
-    qv_out[...] = gqv_ref[0:1, 0 : qv_out.shape[1]]
+    qv_out[...] = gqv_ref[0:1, 0 : qv_out.shape[-1]].reshape(qv_out.shape)
     for ref, out in ((gwo_ref, wo_out), (gwu_ref, wu_out)):
         out[...] = jnp.concatenate([ref[0], ref[1]], axis=1)
     size = gwd_ref.shape[1]
@@ -968,9 +968,9 @@
     total = sm_ref[0] + sm_ref[1] + sm_ref[2] + sm_ref[3]
     for v, out in enumerate((b0_out, b1_out, b2_out, b3_out, b4_out, b5_out)):
         out[...] = total[v : v + 1, 0 : out.shape[1]]
-    for v in range(0, up_out.shape[1], 128):
-        step = min(128, up_out.shape[1] - v)
-        up_out[:, v : v + step] = total[8 + v // 128 : 9 + v // 128, 0:step]
+    size = up_out.shape[-1]
+    pieces = [total[8 + v // 128 : 9 + v // 128, 0 : min(128, size - v)] for v in range(0, size, 128)]
+    up_out[...] = join_lanes(pieces).reshape(up_out.shape)
 
 
 def finish(shapes, *args):
@@ -1008,7 +1008,7 @@
         n, per, e, ctx, linv, qT, vT, k, x_all, w, gctx,
         gwo.reshape(wo.shape), gwu.reshape(wu.shape), gwd.reshape(wd.shape), small,
     )
-    one = lambda a: (1, a.shape[0])
+    one = lambda a: (1, a.shape[0]) if a.shape[0] <= 128 else a.shape
     shapes = (
         tokens.shape[1:], qkv_weight.shape, one(qv_bias), out_weight.shape, one(out_bias), one(norm_gain),
         one(norm_shift), up_weight.shape, one(up_bias), down_weight.shape[::-1], one(down_bias), one(final_gain), one(final_shift),

time: 135 us -> 134 us (level)
  no operation moved by 1% of the time
where the time goes in v5:
time: 134 us; the launch traced here: 133 us
  Pallas kernels  131 us (98%)
  between operations  1.49 us (1%)
    pallas_call x1, Pallas kernels, revisit(): pl.pallas_call(functools.partial(revisit_kernel, n, per), grid=(2 * sourc...  55.5 us
    pallas_call x1, Pallas kernels, attend(): pl.pallas_call(functools.partial(attend_kernel, n), grid=(2 * sources,),...  54.3 us
    pallas_call x1, Pallas kernels, middle(): pl.pallas_call(functools.partial(middle_kernel, n), in_specs=[pl.BlockSpe...  18 us
    pallas_call x1, Pallas kernels, finish(): pl.pallas_call(finish_kernel, in_specs=[vmem] * len(args), out_specs=[vme...  3.38 us

profile of v5, /device:TPU:0, one launch (start us, length us, event | category | flops | bytes accessed | tf_op | source)
XLA Modules:
  0.0 132.7 jit_solution(4182936595889449512)
XLA Ops:
  1.3 54.3 %attend.1 = (bf16[4,256,384]{2,1,0:T(8,128)(2,1)}, f32[4,2,256,192]{3,2,1,0:T(8,128)}, bf16[3,2048,2048]{2,1,0:T(8,128)(2,1)}, bf16[2048,192]{1,0:T(8,128)(2,1)}...) custom-call(s32[1]{0:T(128)S(6)} %copy.29.len_ref, ...), custom_call_target="tpu_custom_call" | custom-call | tf_op jit(solution)/shard_map/attend/pallas_call | solution.py:335
  55.6 18.0 %middle.1 = (bf16[512,768]{1,0:T(8,128)(2,1)}, bf16[4,256,384]{2,1,0:T(8,128)(2,1)}, f32[512,768]{1,0:T(8,128)}, bf16[768,768]{1,0:T(8,128)(2,1)}, bf16[768,768]...) custom-call(s32[1]{0:T(128)S(6)} %copy.29.len_ref, ...), custom_call_target="tpu_custom_call" | custom-call | tf_op jit(solution)/shard_map/middle/pallas_call | solution.py:921
  73.6 55.5 %revisit.1 = (bf16[4,256,384]{2,1,0:T(8,128)(2,1)}, bf16[4,24,576]{2,1,0:T(8,128)(2,1)}, f32[8,256]{1,0:T(8,128)}, f32[2,96,384]{2,1,0:T(8,128)}, f32[2,96,384]{...) custom-call(bf16[3,2048,2048]{2,1,0:T(8,128)(2,1)} %get-tuple-element.60.e_ref, ...), custom_call_target="tpu_custom_call" | custom-call | tf_op jit(solution)/shard_map/revisit/pallas_call | solution.py:732
  129.2 3.4 %finish.1 = (bf16[512,768]{1,0:T(8,128)(2,1)}, f32[96,576]{1,0:T(8,128)}, f32[192]{0:T(256)}, f32[96,768]{1,0:T(8,128)}, f32[1,96]{1,0:T(1,128)}, /*index=5*/f32...) custom-call(bf16[4,256,384]{2,1,0:T(8,128)(2,1)} %get-tuple-element., ...), custom_call_target="tpu_custom_call" | custom-call | tf_op jit(solution)/shard_map/finish/pallas_call | solution.py:978
